TPU v7x, 512 devices: a whole 4x4x16 slice. The times are simulated.
512 devices in a mesh: chan: 8 (over y, x_lo), tile: 64 (over z, x_hi, core).
Axes of the slice: x: 4 (x_hi: 2, x_lo: 2; x = x_hi * 2 + x_lo), y: 4, z: 16, core: 2. Of those that a mesh axis runs over, the one named last changes fastest.
Arguments:
- image: bfloat16 [256, 1024, 256], P('chan', 'tile'), may hold values from -6 to 6
- w_down: bfloat16 [2, 2, 256, 512], P(None, None, None, 'chan'), may hold values from -0.1875 to 0.1875
- w_mix: bfloat16 [3, 3, 512, 512], P(None, None, None, 'chan'), may hold values from -0.09375 to 0.09375
- cotangent: bfloat16 [512, 512, 128], P('chan', 'tile'), may hold values from -6 to 6
Outputs:
- mixed: bfloat16 [512, 512, 128], P('chan', 'tile')
- grad_mix: float32 [512, 3, 3, 512], P('tile', None, None, 'chan')
- grad_down: float32 [256, 2, 2, 512], P('tile', None, None, 'chan')
- grad_image: bfloat16 [256, 1024, 256], P('chan', 'tile')
All inputs are finite; a program needn't handle non-finite values.
Results may differ from a plain program's by a relative error of at most 0.0049.
Values may be sent and summed in bfloat16 or wider, within the bound.
No kernel may reach another device: no remote copies, remote signals or barrier semaphores. Data moves between devices by JAX's collectives and lax.ppermute only.
A program may use at most 64 MiB of HBM per device.

v0:
```python
import math

import jax
import jax.numpy as jnp
from jax import lax
from jax.sharding import PartitionSpec as P


def with_halo(block, sides, width):
    for axis, dim in sides:
        count = lax.axis_size(axis)
        forward = [(i, i + 1) for i in range(count - 1)]
        backward = [(target, source) for source, target in forward]
        low = lax.ppermute(
            lax.slice_in_dim(block, block.shape[dim] - width, None, axis=dim), axis, forward
        )
        high = lax.ppermute(lax.slice_in_dim(block, 0, width, axis=dim), axis, backward)
        block = jnp.concatenate([low, block, high], axis=dim)
    return block


def normal_cdf(value):
    return 0.5 * (1.0 + jax.scipy.special.erf(value / math.sqrt(2.0)))


def normal_pdf(value):
    return jnp.exp(-0.5 * value * value) / math.sqrt(2.0 * math.pi)


def per_device(image, w_down, w_mix, cotangent):
    n_tile = lax.axis_size("tile")
    own_out = cotangent.shape[0]
    n_rows = cotangent.shape[1]
    n_cols = cotangent.shape[2]
    own_in = image.shape[0]
    scale = 1.0 / math.sqrt(n_rows * n_tile * n_cols)
    wide_image = lax.all_gather(image, "chan", axis=0, tiled=True)
    in_chan = wide_image.shape[0]
    patches = wide_image.reshape(in_chan, n_rows, 2, n_cols, 2)
    preact = jnp.einsum("crawb,abcd->drw", patches, w_down, preferred_element_type=jnp.float32)
    hidden = (preact * normal_cdf(preact)).astype(jnp.bfloat16)
    plain = lax.all_gather(hidden, "chan", axis=0, tiled=True)
    full_hidden = with_halo(plain, (("tile", 1),), 1)
    hidden_pad = jnp.pad(full_hidden, ((0, 0), (0, 0), (1, 1)))
    all_chan = hidden_pad.shape[0]
    mixed_sum = jnp.zeros((own_out, n_rows, n_cols), jnp.float32)
    for tap_row in range(3):
        for tap_col in range(3):
            window = hidden_pad[:, tap_row : tap_row + n_rows, tap_col : tap_col + n_cols]
            mixed_sum = mixed_sum + jnp.einsum(
                "crw,cd->drw", window, w_mix[tap_row, tap_col], preferred_element_type=jnp.float32
            )
    mixed = mixed_sum.astype(jnp.bfloat16)
    cot_rimmed = with_halo(cotangent, (("tile", 1),), 1)
    part = hidden_pad
    terms = []
    for tap_row in range(3):
        for tap_col in range(3):
            window = part[:, tap_row : tap_row + n_rows, tap_col : tap_col + n_cols]
            terms.append(
                jnp.einsum("crw,drw->cd", window, cotangent, preferred_element_type=jnp.float32)
            )
    grad_mix = (
        lax.psum_scatter(
            jnp.stack(terms, 1).reshape(all_chan // n_tile * lax.axis_size("tile"), 3, 3, own_out),
            "tile",
            scatter_dimension=0,
            tiled=True,
        )
        * scale
    )
    cot_pad = jnp.pad(cot_rimmed, ((0, 0), (0, 0), (1, 1)))
    total = jnp.zeros((own_out * lax.axis_size("chan"), n_rows, n_cols), jnp.float32)
    for tap_row in range(3):
        for tap_col in range(3):
            back = cot_pad[
                :, 2 - tap_row : 2 - tap_row + n_rows, 2 - tap_col : 2 - tap_col + n_cols
            ]
            filters = w_mix[tap_row, tap_col]
            total = total + jnp.einsum(
                "drw,cd->crw", back, filters, preferred_element_type=jnp.float32
            )
    grad_hidden = lax.psum_scatter(total, "chan", scatter_dimension=0, tiled=True)
    slope = normal_cdf(preact) + preact * normal_pdf(preact)
    grad_pre = (grad_hidden * slope).astype(jnp.bfloat16)
    part = patches
    grad_down = (
        lax.psum_scatter(
            jnp.einsum("crawb,drw->cabd", part, grad_pre, preferred_element_type=jnp.float32),
            "tile",
            scatter_dimension=0,
            tiled=True,
        )
        * scale
    )
    down_turned = lax.all_to_all(w_down, "chan", split_axis=2, concat_axis=3, tiled=True)
    filters = down_turned
    term = jnp.einsum(
        "drw,abcd->crawb",
        lax.all_gather(grad_pre, "chan", axis=0, tiled=True),
        filters,
        preferred_element_type=jnp.float32,
    )
    grad_image = term.reshape(jnp.zeros((own_in, 2 * n_rows, 2 * n_cols), jnp.float32).shape)
    return (mixed, grad_mix, grad_down, grad_image.astype(jnp.bfloat16))


def solution(mesh):
    return jax.shard_map(
        per_device,
        mesh=mesh,
        in_specs=(
            P("chan", "tile", None),
            P(None, None, None, "chan"),
            P(None, None, None, "chan"),
            P("chan", "tile", None),
        ),
        out_specs=(
            P("chan", "tile", None),
            P("tile", None, None, "chan"),
            P("tile", None, None, "chan"),
            P("chan", "tile", None),
        ),
        check_vma=False,
    )
```

profile of v0, /device:TPU:16, one launch (start us, length us, event | category | flops | bytes accessed | tf_op | source)
XLA Modules:
  0.0 1002.9 jit_solution(11535265165605964177)
XLA Ops:
  8.9 1.7 collective-permute-start.2
  11.9 1.4 fusion.96
  13.4 3.2 collective-permute-done.3
  20.2 2.6 bitcast_add_fusion
  22.9 49.6 %all-gather.4.cloned.1.call-done = bf16[256,16,256]{2,1,0:T(8,128)(2,1)} async-done(((bf16[32,16,256]{2,1,0:T(8,128)(2,1)}), bf16[256,16,256]{2,1,0:T(8,128)(2,1)}) %all-gather.4.cloned.1.call-update) | async-done | bytes 2097168 | tf_op jit(solution)/shard_map/all_gather | solution.py:37
  72.5 3.0 copy.69
  75.5 2.2 reshape.16
  77.7 2.5 fusion.11
  80.2 54.6 %reduce-scatter.5.cloned.1.call-done = f32[64,8,128]{2,0,1:T(8,128)} async-done(((f32[512,8,128]{2,0,1:T(8,128)}), f32[64,8,128]{2,0,1:T(8,128)}) %reduce-scatter.5.cloned.1.call-update) | async-done | bytes 262160 | tf_op jit(solution)/shard_map/reduce_scatter | solution.py:83
  134.8 1.7 fusion.66
  140.3 5.5 all-to-all-start
  147.7 2.4 all-to-all-done
  150.8 512.4 %all-reduce.5.cloned.1.call-done = f32[256,2,2,64]{3,2,1,0:T(2,128)} async-done(((f32[256,2,2,64]{3,2,1,0:T(2,128)}), f32[256,2,2,64]{3,2,1,0:T(2,128)}) %all-reduce.5.cloned.1.call-update) | async-done | bytes 262160
  663.1 1.3 dynamic-slice_multiply_fusion
  664.4 46.0 %all-gather.6.cloned.1.call-done = bf16[512,8,128]{2,0,1:T(8,128)(2,1)} async-done(((bf16[64,8,128]{2,0,1:T(8,128)(2,1)}), bf16[512,8,128]{2,0,1:T(8,128)(2,1)}) %all-gather.6.cloned.1.call-update) | async-done | bytes 1048592 | tf_op jit(solution)/shard_map/all_gather | solution.py:42
  710.4 1.6 fusion.138
  712.0 1.4 collective-permute-start
  713.5 1.5 collective-permute-start.1
  714.9 45.3 %all-gather.8.cloned.1.call-done = bf16[512,8,128]{2,0,1:T(8,128)(2,1)} async-done(((bf16[64,8,128]{2,0,1:T(8,128)(2,1)}), bf16[512,8,128]{2,0,1:T(8,128)(2,1)}) %all-gather.8.cloned.1.call-update) | async-done | bytes 1048592 | tf_op jit(solution)/shard_map/all_gather | solution.py:100
  760.2 1.5 fusion.10
  764.7 2.9 fusion.5
  776.4 2.9 copy.80
  783.4 211.3 %reduce-scatter.3.cloned.1.call-done = f32[8,3,3,64]{3,0,2,1:T(8,128)} async-done(((f32[512,3,3,64]{3,0,2,1:T(8,128)}), f32[8,3,3,64]{3,0,2,1:T(8,128)}) %reduce-scatter.3.cloned.1.call-update) | async-done | bytes 18448 | tf_op jit(solution)/shard_map/reduce_scatter | solution.py:64
  994.6 1.4 broadcast_multiply_fusion
  (85 shorter events, 27.7 us)
Async XLA Ops:
  7.2 9.6 copy-start.5
  7.2 65.3 %all-gather.4.cloned.1.call-start = ((), (), s32[]{:S(2)}) async-start(), calls=%async_computation.3 | async-start | bytes 2359296 | tf_op jit(solution)/shard_map/all_gather | solution.py:37
  7.9 126.9 %reduce-scatter.5.cloned.1.call-start = ((), (), s32[]{:S(2)}) async-start(), calls=%async_computation.6 | async-start | bytes 2359296 | tf_op jit(solution)/shard_map/reduce_scatter | solution.py:83
  8.9 4.5 collective-permute-start.2
  10.6 5.9 collective-permute-start.3
  22.8 640.3 %all-reduce.5.cloned.1.call-start = ((), (), s32[]{:S(2)}) async-start(), calls=%async_computation.8 | async-start | bytes 1048576
  75.5 2.2 copy-start.12
  77.7 58.9 %copy-start.6 = (bf16[256,8,2,128,2]{0,4,3,2,1:T(2,128)(2,1)S(1)}, bf16[256,8,2,128,2]{0,4,3,2,1:T(2,128)(2,1)}, u32[]{:S(2)}) copy-start(bf16[256,8,2,128,2]{0,4,3,2,1:T(2,128)(2,1)} %reshape.16) | copy-start | bytes 6291460
  136.6 2.1 copy-start.11
  138.1 572.3 %all-gather.6.cloned.1.call-start = ((), (), s32[]{:S(2)}) async-start(), calls=%async_computation.4 | async-start | bytes 1179648 | tf_op jit(solution)/shard_map/all_gather | solution.py:42
  138.7 621.6 %all-gather.8.cloned.1.call-start = ((), (), s32[]{:S(2)}) async-start(), calls=%async_computation.7 | async-start | bytes 1179648 | tf_op jit(solution)/shard_map/all_gather | solution.py:100
  140.3 9.9 all-to-all-start
  145.8 848.8 %reduce-scatter.3.cloned.1.call-start = ((), (), s32[]{:S(2)}) async-start(), calls=%async_computation.5 | async-start | bytes 2396160 | tf_op jit(solution)/shard_map/reduce_scatter | solution.py:64
  712.0 51.7 %copy-start = (bf16[512,8,128]{2,0,1:T(8,128)(2,1)S(1)}, bf16[512,8,128]{2,0,1:T(8,128)(2,1)}, u32[]{:S(2)}) copy-start(bf16[512,8,128]{2,0,1:T(8,128)(2,1)} %all-gather.6.cloned.1.call-done) | copy-start | bytes 3145732
  712.0 52.0 %collective-permute-start = (bf16[512,1,128]{2,0,1:T(8,128)(2,1)}, bf16[512,1,128]{2,0,1:T(8,128)(2,1)S(1)}, u32[]{:S(2)}, u32[]{:S(2)}) collective-permute-start(bf16[512,1,128]{2,0,1:T(8,128)(2,1)} %get-tuple-element.18), channel_id=1, source_target_pairs={{0,1},{1,2},{2,3},{3,4},{4,5},{5,6},{6,7},{7,8},{8,9},{9,10},{10,1... | collective-permute-start | bytes 393224 | tf_op jit(solution)/shard_map/ppermute | solution.py:14
  713.5 51.3 %collective-permute-start.1 = (bf16[512,1,128]{2,0,1:T(8,128)(2,1)S(1)}, bf16[512,1,128]{2,0,1:T(8,128)(2,1)}, u32[]{:S(2)}, u32[]{:S(2)}) collective-permute-start(bf16[512,1,128]{2,0,1:T(8,128)(2,1)S(1)} %get-tuple-element.19), channel_id=1, source_target_pairs={{1,0},{2,1},{3,2},{4,3},{5,4},{6,5},{7,6},{8,7},{9,8},{10,9},{11,1... | collective-permute-start | bytes 393224 | tf_op jit(solution)/shard_map/ppermute | solution.py:17
  764.0 3.6 copy-start.4
  764.1 4.1 copy-start.1
  764.1 0.7 copy-start.9
  764.7 3.4 copy-start.10
  773.3 1.0 copy-start.2
  775.4 1.0 copy-start.7
  779.3 1.3 copy-start.3
  780.6 1.2 copy-start.8
Sparse Core Ops, SparseCore 0:
  10.1 62.3 all-gather.3
  75.3 59.4 reduce-scatter.4
  138.2 524.8 all-reduce.4
  665.9 44.4 all-gather.5
  712.5 47.6 all-gather.7
  779.4 215.1 reduce-scatter.2
where the time goes:
time: 1000 us
  waiting for transfers between devices  927 us (93%)
  local copies, waits for them, and re-layouts  21.7 us (2%)
  matrix products  20.4 us (2%)
  between operations  15.2 us (2%)
  starting transfers between devices  11.6 us (1%)
    unnamed x7, waiting for transfers between devices  514 us
    reduce_scatter x1, waiting for transfers between devices, per_device(): lax.psum_scatter(jnp.stack(terms, 1).reshape(all_chan // n_tile * lax.axi...  211 us
    reduce_scatter x1, waiting for transfers between devices, per_device(): lax.psum_scatter(total, 'chan', scatter_dimension=0, tiled=True)  54.6 us
    all_gather x1, waiting for transfers between devices, per_device(): wide_image = lax.all_gather(image, 'chan', axis=0, tiled=True)  49.6 us
    all_gather x1, waiting for transfers between devices, per_device(): plain = lax.all_gather(hidden, 'chan', axis=0, tiled=True)  46 us
    all_gather x1, waiting for transfers between devices, per_device(): lax.all_gather(grad_pre, 'chan', axis=0, tiled=True)  45.3 us
  transfers between devices with their start and end apart: 11, of which 8 were waited for; matrix products, arithmetic and copies ran while one was open for 3% of the time, Pallas kernels for 0%

commit v1 on v0

v1 whole, which is shorter than its diff:
```python
import math

import jax
import jax.numpy as jnp
from jax import lax
from jax.experimental import pallas as pl
from jax.experimental.pallas import tpu as pltpu
from jax.sharding import Mesh, PartitionSpec as P

TILE = ("z", "xh", "core")
BF16 = jnp.bfloat16
F32 = jnp.float32


def normal_cdf(value):
    return 0.5 * (1.0 + jax.scipy.special.erf(value / math.sqrt(2.0)))


def normal_pdf(value):
    return jnp.exp(-0.5 * value * value) / math.sqrt(2.0 * math.pi)


def dot(spec, left, right):
    return jnp.einsum(spec, left, right, preferred_element_type=F32)


def swap(block, axis):
    return lax.all_to_all(block, axis, 0, 0)


def spread(block):
    count = lax.axis_size("chan")
    return swap(jnp.broadcast_to(block[None], (count,) + block.shape), "chan")


def halved(block, axis):
    mine = lax.axis_index(axis)
    keep = lax.dynamic_index_in_dim(block, mine, 0, keepdims=False)
    give = lax.dynamic_index_in_dim(block, 1 - mine, 0, keepdims=False).astype(BF16)
    return keep + lax.ppermute(give, axis, [(0, 1), (1, 0)]).astype(F32)


def mixed_kernel(mix_ref, hidden_ref, inner_ref, up_ref, down_ref):
    n_rows, _, n_cols = hidden_ref.shape
    own_out = inner_ref.shape[1]
    column = lax.broadcasted_iota(jnp.int32, (3, own_out, n_cols), 2)
    sums = [jnp.zeros((own_out, n_cols), F32) for _ in range(n_rows + 2)]
    for row in range(n_rows):
        heap = jnp.dot(mix_ref[...], hidden_ref[row], preferred_element_type=F32)
        heap = heap.reshape(3, 3, own_out, n_cols)
        left = jnp.where(column > 0, pltpu.roll(heap[:, 0], 1, 2), 0.0)
        right = jnp.where(column < n_cols - 1, pltpu.roll(heap[:, 2], n_cols - 1, 2), 0.0)
        line = left + heap[:, 1] + right
        for tap_row in range(3):
            sums[row + 2 - tap_row] = sums[row + 2 - tap_row] + line[tap_row]
    up_ref[...] = sums[0]
    down_ref[...] = sums[n_rows + 1]
    for row in range(n_rows):
        inner_ref[row] = sums[row + 1]


def mixed_parts(mix, hidden):
    n_rows, _, n_cols = hidden.shape
    own_out = mix.shape[0] // 9
    whole = pl.BlockSpec(memory_space=pltpu.VMEM)
    edge = jax.ShapeDtypeStruct((own_out, n_cols), F32)
    return pl.pallas_call(
        mixed_kernel,
        out_shape=(jax.ShapeDtypeStruct((n_rows, own_out, n_cols), F32), edge, edge),
        in_specs=[whole, whole],
        out_specs=(whole, whole, whole),
        cost_estimate=pl.CostEstimate(
            flops=2 * mix.size * n_rows * n_cols,
            bytes_accessed=2 * (mix.size + hidden.size) + 4 * n_rows * own_out * n_cols,
            transcendentals=0,
        ),
        compiler_params=pltpu.CompilerParams(vmem_limit_bytes=32 << 20),
    )(mix, hidden)


def per_device(image, w_down, w_mix, cotangent):
    n_chan = lax.axis_size("chan")
    n_tile = lax.axis_size(TILE)
    own_in, _, in_cols = image.shape
    own_out, n_rows, n_cols = cotangent.shape
    all_out = n_chan * own_out
    taps = 4 * own_in
    scale = 1.0 / math.sqrt(n_rows * n_tile * n_cols)
    chan = lax.axis_index("chan")
    ahead = [(i, i + 1) for i in range(n_tile - 1)]
    back = [(i + 1, i) for i in range(n_tile - 1)]

    cot = jnp.transpose(cotangent, (1, 0, 2))
    above = lax.ppermute(cot[n_rows - 1 :], TILE, ahead)
    below = lax.ppermute(cot[:1], TILE, back)
    rim = jnp.concatenate([above, cot, below], axis=0)
    rim = jnp.pad(rim, ((0, 0), (0, 0), (1, 1)))
    shifted = jnp.stack([rim[:, :, 2 - j : 2 - j + n_cols] for j in range(3)], axis=1)
    cols = jnp.stack(
        [
            jnp.concatenate([shifted[r + 2 - i] for i in range(3)]).reshape(9 * own_out, n_cols)
            for r in range(n_rows)
        ]
    )

    mix = jnp.transpose(w_mix, (0, 1, 3, 2)).reshape(9 * own_out, all_out)

    even_odd = (
        jnp.arange(in_cols)[:, None, None]
        == 2 * jnp.arange(n_cols)[None, None, :] + jnp.arange(2)[None, :, None]
    ).astype(BF16)
    own_patches = dot("crax,xbw->rcabw", image.reshape(own_in, n_rows, 2, in_cols), even_odd)
    own_patches = own_patches.astype(BF16).reshape(n_rows, taps, n_cols)
    down = w_down.reshape(2, 2, n_chan, own_in, own_out)
    down = jnp.transpose(down, (2, 4, 3, 0, 1)).reshape(n_chan * own_out, taps)

    sent = jnp.concatenate(
        [jnp.broadcast_to(down[None], (n_chan,) + down.shape), own_patches], axis=1
    )
    partial = dot("kc,rkw->rcw", mix, cols).astype(BF16)
    got, partial = lax.optimization_barrier((swap(sent, "chan"), partial))
    all_down = got[:, : n_chan * own_out].reshape(n_chan, n_chan, own_out, taps)
    patches = got[:, n_chan * own_out :]
    preact = dot("sjdk,jkw->sdw", all_down, patches).reshape(all_out, n_cols)
    cdf = normal_cdf(preact)
    hidden = spread((preact * cdf).astype(BF16))

    grad_hidden = jnp.sum(swap(partial, "chan").astype(F32), axis=0)
    slope = cdf + preact * normal_pdf(preact)
    grad_pre = spread((grad_hidden * slope).astype(BF16))

    n_z, n_xh, n_core = (lax.axis_size(a) for a in TILE)
    rows = all_out // n_tile
    grad_mix = dot("rcw,rkw->ck", hidden, cols).reshape(n_z, n_xh, n_core, rows, 9 * own_out)
    grad_mix = halved(jnp.transpose(grad_mix, (2, 1, 0, 3, 4)), "core")
    grad_mix = halved(grad_mix, "xh")

    inner, up, down = mixed_parts(mix, hidden)
    from_below = lax.ppermute(up, TILE, back)
    from_above = lax.ppermute(down, TILE, ahead)
    edges = jnp.zeros_like(inner).at[0].set(from_above).at[n_rows - 1].set(from_below)
    mixed = jnp.transpose((inner + edges).astype(BF16), (1, 0, 2))

    grad_down = dot("rkw,rdw->kd", own_patches, grad_pre)
    groups = n_tile // n_chan
    lanes = 2 * own_out
    lines_of = taps * own_out // groups // lanes
    grad_down = grad_down.reshape(groups, 2, lines_of, n_chan, own_out)
    grad_down = jnp.transpose(grad_down, (0, 3, 2, 1, 4))
    grad_down = grad_down.reshape(n_z, n_xh, n_core, lines_of, lanes)
    grad_down = halved(jnp.transpose(grad_down, (2, 1, 0, 3, 4)), "core")
    grad_down = halved(grad_down, "xh")
    total = jnp.concatenate([grad_mix, grad_down], axis=-1).astype(BF16)
    total = jnp.sum(swap(total, "z").astype(F32), axis=0) * scale
    grad_mix = total[:, : 9 * own_out].reshape(rows, 3, 3, own_out)
    piece = total[:, 9 * own_out :]
    perm = [
        (k * n_tile + g * n_chan + to, to * n_tile + k * groups + g)
        for k in range(n_chan)
        for g in range(groups)
        for to in range(n_chan)
    ]
    piece = lax.ppermute(piece, ("chan",) + TILE, perm)
    grad_down = jnp.transpose(piece.reshape(lines_of, 2, own_out), (1, 0, 2))
    grad_down = grad_down.reshape(taps // groups // 4, 2, 2, own_out)

    turned = lax.dynamic_index_in_dim(all_down, chan, 1, keepdims=False).reshape(all_out, taps)
    grad_image = dot("dk,rdw->rkw", turned, grad_pre).astype(BF16)
    grad_image = dot(
        "rcabw,xbw->crax", grad_image.reshape(n_rows, own_in, 2, 2, n_cols), even_odd
    )
    grad_image = grad_image.astype(BF16).reshape(image.shape)
    return (mixed, grad_mix, grad_down, grad_image)


def solution(mesh):
    grid = mesh.devices
    n_chan, n_tile = grid.shape
    split = Mesh(grid.reshape(n_chan, n_tile // 4, 2, 2), ("chan",) + TILE)
    return jax.shard_map(
        per_device,
        mesh=split,
        in_specs=(
            P("chan", TILE, None),
            P(None, None, None, "chan"),
            P(None, None, None, "chan"),
            P("chan", TILE, None),
        ),
        out_specs=(
            P("chan", TILE, None),
            P(TILE, None, None, "chan"),
            P(TILE, None, None, "chan"),
            P("chan", TILE, None),
        ),
        check_vma=False,
    )
```

time: 1000 us -> 174 us (0.17)
  the two profiles are of different devices: /device:TPU:16 before, /device:TPU:56 now
where the time goes in v1:
time: 174 us; the launch traced here: 173 us
  starting transfers between devices  71.7 us (41%)
  waiting for transfers between devices  57.7 us (33%)
  blocking collectives  14.8 us (9%)
  local copies, waits for them, and re-layouts  14.2 us (8%)
  matrix products  7.14 us (4%)
  other arithmetic  4.56 us (3%)
    all_to_all x4, waiting for transfers between devices, swap(): return lax.all_to_all(block, axis, 0, 0)  38.1 us
    all_to_all x4, starting transfers between devices, swap(): return lax.all_to_all(block, axis, 0, 0)  34.8 us
    ppermute x4, starting transfers between devices, halved(): return keep + lax.ppermute(give, axis, [(0, 1), (1, 0)]).astype(F32)  15.9 us
    all_to_all x1, blocking collectives, swap(): return lax.all_to_all(block, axis, 0, 0)  14.8 us
    ppermute x1, waiting for transfers between devices, per_device(): piece = lax.ppermute(piece, ('chan',) + TILE, perm)  12.2 us
    ppermute x4, waiting for transfers between devices, halved(): return keep + lax.ppermute(give, axis, [(0, 1), (1, 0)]).astype(F32)  7.39 us
    dot_general x7, matrix products, dot(): return jnp.einsum(spec, left, right, preferred_element_type=F32)  7.14 us
    ppermute x1, starting transfers between devices, per_device(): from_below = lax.ppermute(up, TILE, back)  6.05 us
  transfers between devices with their start and end apart: 13, of which 6 were waited for; matrix products, arithmetic and copies ran while one was open for 10% of the time, Pallas kernels for 1%

profile of v1, /device:TPU:56, one launch (start us, length us, event | category | flops | bytes accessed | tf_op | source)
XLA Modules:
  0.0 172.7 jit_solution(6240878566088968658)
XLA Ops:
  1.6 1.9 %collective-permute-start = (bf16[1,64,128]{2,1,0:T(8,128)(2,1)S(1)}, bf16[1,64,128]{2,1,0:T(8,128)(2,1)S(1)}, u32[]{:S(2)}, u32[]{:S(2)}) collective-permute-start(bf16[1,64,128]{2,1,0:T(8,128)(2,1)S(1)} %get-tuple-element.70), channel_id=1, source_target_pairs={{0,1},{1,2},{2,3},{3,4},{4,5},{5,6},{6,7},{7,8},{8,9},{9,10},{10,1... | collective-permute-start | bytes 49160 | tf_op jit(solution)/shard_map/ppermute | solution.py:94
  3.5 6.0 %collective-permute-start.1 = (bf16[1,64,128]{2,1,0:T(8,128)(2,1)S(1)}, bf16[1,64,128]{2,1,0:T(8,128)(2,1)S(1)}, u32[]{:S(2)}, u32[]{:S(2)}) collective-permute-start(bf16[1,64,128]{2,1,0:T(8,128)(2,1)S(1)} %get-tuple-element.71), channel_id=1, source_target_pairs={{1,0},{2,1},{3,2},{4,3},{5,4},{6,5},{7,6},{8,7},{9,8},{10,9},{11,1... | collective-permute-start | bytes 49160 | tf_op jit(solution)/shard_map/ppermute | solution.py:95
  13.1 5.6 %all-to-all-start = ((bf16[8,640,128]{2,1,0:T(8,128)(2,1)}), bf16[8,640,128]{2,1,0:T(8,128)(2,1)S(1)}, u32[]{:S(2)}, u32[]{:S(2)}) async-start(bf16[8,640,128]{2,1,0:T(8,128)(2,1)} %pad_maximum_fusion), calls=%async_computation | async-start | bytes 2621440 | tf_op jit(solution)/shard_map/all_to_all | solution.py:28
  20.4 2.0 %fusion = bf16[8,512,128]{1,2,0:T(8,128)(2,1)} fusion(bf16[8,576,128]{2,1,0:T(8,128)(2,1)S(1)} %bitcast_dynamic-update-slice_fusion, bf16[576,512,1]{1,0,2:T(8,128)(2,1)S(1)} %bitcast.172), kind=kOutput, calls=%fused_computation.2 | convolution fusion | flops 604504064 | bytes 2818048 | tf_op jit(solution)/shard_map/kc,rkw->rcw/dot_general | solution.py:24
  22.4 11.2 %all-to-all-done = bf16[8,640,128]{2,1,0:T(8,128)(2,1)S(1)} async-done(((bf16[8,640,128]{2,1,0:T(8,128)(2,1)}), bf16[8,640,128]{2,1,0:T(8,128)(2,1)S(1)}, u32[]{:S(2)}, u32[]{:S(2)}) %all-to-all-start) | async-done | bytes 1310752 | tf_op jit(solution)/shard_map/all_to_all | solution.py:28
  34.7 6.0 %all-to-all-start.2 = ((bf16[8,512,128]{1,2,0:T(8,128)(2,1)}), bf16[8,512,128]{1,2,0:T(8,128)(2,1)}, u32[]{:S(2)}, u32[]{:S(2)}) async-start(bf16[8,512,128]{1,2,0:T(8,128)(2,1)} %fusion), calls=%async_computation.2 | async-start | bytes 2097152 | tf_op jit(solution)/shard_map/all_to_all | solution.py:28
  42.1 10.1 %all-to-all-done.2 = bf16[8,512,128]{1,2,0:T(8,128)(2,1)} async-done(((bf16[8,512,128]{1,2,0:T(8,128)(2,1)}), bf16[8,512,128]{1,2,0:T(8,128)(2,1)}, u32[]{:S(2)}, u32[]{:S(2)}) %all-to-all-start.2) | async-done | bytes 1048608 | tf_op jit(solution)/shard_map/all_to_all | solution.py:28
  53.8 1.4 fusion.11
  55.3 14.8 %all_to_all.25 = bf16[8,512,128]{2,1,0:T(8,128)(2,1)} all-to-all(bf16[8,512,128]{2,1,0:T(8,128)(2,1)S(1)} %broadcast_in_dim.11), channel_id=1, replica_groups=mesh['chan'=8,'z'=16,'xh'=2,'core'=2] {'chan'}, dimensions={0} | all-to-all | bytes 2097152 | tf_op jit(solution)/shard_map/all_to_all | solution.py:28
  71.2 5.9 %all-to-all-start.1 = ((bf16[8,512,128]{2,1,0:T(8,128)(2,1)}), bf16[8,512,128]{2,1,0:T(8,128)(2,1)S(1)}, u32[]{:S(2)}, u32[]{:S(2)}) async-start(bf16[8,512,128]{2,1,0:T(8,128)(2,1)} %broadcast_in_dim.10), calls=%async_computation.1 | async-start | bytes 2097152 | tf_op jit(solution)/shard_map/all_to_all | solution.py:28
  77.1 1.9 %convolution_bitcast_fusion.1 = f32[8,8,8,2,64]{4,2,1,3,0:T(8,128)S(1)} fusion(bf16[8,64,8,128,1,1]{3,1,0,2,5,4:T(8,128)(2,1)} %bitcast.176, bf16[8,2,8,8,128,1]{4,3,2,1,0,5:T(8,128)(2,1)S(1)} %bitcast.179), kind=kOutput, calls=%fused_computation.5 | convolution fusion | flops 134217728 | bytes 1572864 | tf_op jit(solution)/shard_map/rkw,rdw->kd/dot_general | solution.py:24
  80.3 1.9 %collective-permute-start.6 = (bf16[2,16,8,128]{3,2,1,0:T(8,128)(2,1)}, bf16[2,16,8,128]{3,2,1,0:T(8,128)(2,1)}, u32[]{:S(2)}, u32[]{:S(2)}) collective-permute-start(bf16[2,16,8,128]{3,2,1,0:T(8,128)(2,1)} %fusion.26), channel_id=1, source_target_pairs={{0,1},{1,0},{2,3},{3,2},{4,5},{5,4},{6,7},{7,6},{8,9},{9,8},{10,11... | collective-permute-start | bytes 196616 | tf_op jit(solution)/shard_map/ppermute | solution.py:40
  82.3 4.6 %all-to-all-done.1.hidden_ref = bf16[8,512,128]{2,1,0:T(8,128)(2,1)S(1)} async-done(((bf16[8,512,128]{2,1,0:T(8,128)(2,1)}), bf16[8,512,128]{2,1,0:T(8,128)(2,1)S(1)}, u32[]{:S(2)}, u32[]{:S(2)}) %all-to-all-start.1) | async-done | bytes 1048608 | tf_op jit(solution)/shard_map/all_to_all | solution.py:28
  86.8 1.5 shard_map.75
  88.3 1.9 %collective-permute-start.2 = (f32[64,128]{1,0:T(8,128)S(1)}, f32[64,128]{1,0:T(8,128)}, u32[]{:S(2)}, u32[]{:S(2)}) collective-permute-start(f32[64,128]{1,0:T(8,128)S(1)} %get-tuple-element.35), channel_id=1, source_target_pairs={{0,1},{1,2},{2,3},{3,4},{4,5},{5,6},{6,7},{7,8},{8,9},{9,10},{10,1... | collective-permute-start | bytes 98312 | tf_op jit(solution)/shard_map/ppermute | solution.py:140
  90.2 6.0 %collective-permute-start.3 = (f32[64,128]{1,0:T(8,128)S(1)}, f32[64,128]{1,0:T(8,128)}, u32[]{:S(2)}, u32[]{:S(2)}) collective-permute-start(f32[64,128]{1,0:T(8,128)S(1)} %get-tuple-element.36), channel_id=1, source_target_pairs={{1,0},{2,1},{3,2},{4,3},{5,4},{6,5},{7,6},{8,7},{9,8},{10,9},{11,1... | collective-permute-start | bytes 98312 | tf_op jit(solution)/shard_map/ppermute | solution.py:139
  97.3 6.5 %collective-permute-start.4 = (bf16[2,16,8,576]{3,2,0,1:T(8,128)(2,1)S(1)}, bf16[2,16,8,576]{3,2,0,1:T(8,128)(2,1)S(1)}, u32[]{:S(2)}, u32[]{:S(2)}) collective-permute-start(bf16[2,16,8,576]{3,2,0,1:T(8,128)(2,1)S(1)} %fusion.4), channel_id=1, source_target_pairs={{0,1},{1,0},{2,3},{3,2},{4,5},{5,4},{6,7},{7,6},{8,9},{9,8},{10,11... | collective-permute-start | bytes 884744 | tf_op jit(solution)/shard_map/ppermute | solution.py:40
  104.8 5.0 %collective-permute-start.7 = (bf16[16,8,128]{2,1,0:T(8,128)(2,1)S(1)}, bf16[16,8,128]{2,1,0:T(8,128)(2,1)S(1)}, u32[]{:S(2)}, u32[]{:S(2)}) collective-permute-start(bf16[16,8,128]{2,1,0:T(8,128)(2,1)S(1)} %fusion.28), channel_id=1, source_target_pairs={{0,2},{2,0},{1,3},{3,1},{4,6},{6,4},{5,7},{7,5},{8,10},{10,8},{9,1... | collective-permute-start | bytes 98312 | tf_op jit(solution)/shard_map/ppermute | solution.py:40
  110.0 2.4 %collective-permute-start.5 = (bf16[16,8,576]{2,1,0:T(8,128)(2,1)S(1)}, bf16[16,8,576]{2,1,0:T(8,128)(2,1)S(1)}, u32[]{:S(2)}, u32[]{:S(2)}) collective-permute-start(bf16[16,8,576]{2,1,0:T(8,128)(2,1)S(1)} %fusion.19), channel_id=1, source_target_pairs={{0,2},{2,0},{1,3},{3,1},{4,6},{6,4},{5,7},{7,5},{8,10},{10,8},{9,1... | collective-permute-start | bytes 442376 | tf_op jit(solution)/shard_map/ppermute | solution.py:40
  112.5 7.4 %collective-permute-done.5 = bf16[16,8,576]{2,1,0:T(8,128)(2,1)S(1)} collective-permute-done((bf16[16,8,576]{2,1,0:T(8,128)(2,1)S(1)}, bf16[16,8,576]{2,1,0:T(8,128)(2,1)S(1)}, u32[]{:S(2)}, u32[]{:S(2)}) %collective-permute-start.5) | collective-permute-done | bytes 147488 | tf_op jit(solution)/shard_map/ppermute | solution.py:40
  120.6 17.3 %all-to-all-start.4 = ((bf16[16,8,704]{2,1,0:T(8,128)(2,1)}), bf16[16,8,704]{2,1,0:T(8,128)(2,1)S(1)}, u32[]{:S(2)}, u32[]{:S(2)}) async-start(bf16[16,8,704]{2,1,0:T(8,128)(2,1)} %pad_maximum_fusion.2), calls=%async_computation.4 | async-start | bytes 393216 | tf_op jit(solution)/shard_map/all_to_all | solution.py:28
  141.0 12.2 %all-to-all-done.4 = bf16[16,8,704]{2,1,0:T(8,128)(2,1)S(1)} async-done(((bf16[16,8,704]{2,1,0:T(8,128)(2,1)}), bf16[16,8,704]{2,1,0:T(8,128)(2,1)S(1)}, u32[]{:S(2)}, u32[]{:S(2)}) %all-to-all-start.4) | async-done | bytes 180256 | tf_op jit(solution)/shard_map/all_to_all | solution.py:28
  153.3 5.0 %collective-permute-start.8 = (f32[8,128]{1,0:T(8,128)S(1)}, f32[8,128]{1,0:T(8,128)S(1)}, u32[]{:S(2)}, u32[]{:S(2)}) collective-permute-start(f32[8,128]{1,0:T(8,128)S(1)} %slice.139), channel_id=1, source_target_pairs={{0,0},{1,64},{2,128},{3,192},{4,256},{5,320},{6,384},{7,448},{8,1}... | collective-permute-start | bytes 12296 | tf_op jit(solution)/shard_map/ppermute | solution.py:163
  159.8 12.2 %collective-permute-done.8 = f32[8,128]{1,0:T(8,128)S(1)} collective-permute-done((f32[8,128]{1,0:T(8,128)S(1)}, f32[8,128]{1,0:T(8,128)S(1)}, u32[]{:S(2)}, u32[]{:S(2)}) %collective-permute-start.8) | collective-permute-done | bytes 4128 | tf_op jit(solution)/shard_map/ppermute | solution.py:163
  (81 shorter events, 20.6 us)
Async XLA Ops:
  0.6 10.5 %copy-start.5 = (bf16[2,2,256,64]{2,3,1,0:T(8,128)(2,1)S(1)}, bf16[2,2,256,64]{2,3,1,0:T(8,128)(2,1)}, u32[]{:S(2)}) copy-start(bf16[2,2,256,64]{2,3,1,0:T(8,128)(2,1)} %param.9) | copy-start | bytes 393220
  1.6 17.1 %collective-permute-start = (bf16[1,64,128]{2,1,0:T(8,128)(2,1)S(1)}, bf16[1,64,128]{2,1,0:T(8,128)(2,1)S(1)}, u32[]{:S(2)}, u32[]{:S(2)}) collective-permute-start(bf16[1,64,128]{2,1,0:T(8,128)(2,1)S(1)} %get-tuple-element.70), channel_id=1, source_target_pairs={{0,1},{1,2},{2,3},{3,4},{4,5},{5,6},{6,7},{7,8},{8,9},{9,10},{10,1... | collective-permute-start | bytes 49160 | tf_op jit(solution)/shard_map/ppermute | solution.py:94
  3.5 15.1 %collective-permute-start.1 = (bf16[1,64,128]{2,1,0:T(8,128)(2,1)S(1)}, bf16[1,64,128]{2,1,0:T(8,128)(2,1)S(1)}, u32[]{:S(2)}, u32[]{:S(2)}) collective-permute-start(bf16[1,64,128]{2,1,0:T(8,128)(2,1)S(1)} %get-tuple-element.71), channel_id=1, source_target_pairs={{1,0},{2,1},{3,2},{4,3},{5,4},{6,5},{7,6},{8,7},{9,8},{10,9},{11,1... | collective-permute-start | bytes 49160 | tf_op jit(solution)/shard_map/ppermute | solution.py:95
  13.1 20.6 %all-to-all-start = ((bf16[8,640,128]{2,1,0:T(8,128)(2,1)}), bf16[8,640,128]{2,1,0:T(8,128)(2,1)S(1)}, u32[]{:S(2)}, u32[]{:S(2)}) async-start(bf16[8,640,128]{2,1,0:T(8,128)(2,1)} %pad_maximum_fusion), calls=%async_computation | async-start | bytes 2621440 | tf_op jit(solution)/shard_map/all_to_all | solution.py:28
  19.2 1.2 copy-start
  19.4 1.0 copy-start.3
  33.6 1.1 copy-start.1
  34.7 17.5 %all-to-all-start.2 = ((bf16[8,512,128]{1,2,0:T(8,128)(2,1)}), bf16[8,512,128]{1,2,0:T(8,128)(2,1)}, u32[]{:S(2)}, u32[]{:S(2)}) async-start(bf16[8,512,128]{1,2,0:T(8,128)(2,1)} %fusion), calls=%async_computation.2 | async-start | bytes 2097152 | tf_op jit(solution)/shard_map/all_to_all | solution.py:28
  71.2 15.6 %all-to-all-start.1 = ((bf16[8,512,128]{2,1,0:T(8,128)(2,1)}), bf16[8,512,128]{2,1,0:T(8,128)(2,1)S(1)}, u32[]{:S(2)}, u32[]{:S(2)}) async-start(bf16[8,512,128]{2,1,0:T(8,128)(2,1)} %broadcast_in_dim.10), calls=%async_computation.1 | async-start | bytes 2097152 | tf_op jit(solution)/shard_map/all_to_all | solution.py:28
  79.7 16.6 %copy-start.4 = (bf16[8,576,128]{2,1,0:T(8,128)(2,1)S(1)}, bf16[8,576,128]{2,1,0:T(8,128)(2,1)}, u32[]{:S(2)}) copy-start(bf16[8,576,128]{2,1,0:T(8,128)(2,1)} %copy-done.3) | copy-start | bytes 3538948
  80.3 23.6 %collective-permute-start.6 = (bf16[2,16,8,128]{3,2,1,0:T(8,128)(2,1)}, bf16[2,16,8,128]{3,2,1,0:T(8,128)(2,1)}, u32[]{:S(2)}, u32[]{:S(2)}) collective-permute-start(bf16[2,16,8,128]{3,2,1,0:T(8,128)(2,1)} %fusion.26), channel_id=1, source_target_pairs={{0,1},{1,0},{2,3},{3,2},{4,5},{5,4},{6,7},{7,6},{8,9},{9,8},{10,11... | collective-permute-start | bytes 196616 | tf_op jit(solution)/shard_map/ppermute | solution.py:40
  88.3 51.1 %collective-permute-start.2 = (f32[64,128]{1,0:T(8,128)S(1)}, f32[64,128]{1,0:T(8,128)}, u32[]{:S(2)}, u32[]{:S(2)}) collective-permute-start(f32[64,128]{1,0:T(8,128)S(1)} %get-tuple-element.35), channel_id=1, source_target_pairs={{0,1},{1,2},{2,3},{3,4},{4,5},{5,6},{6,7},{7,8},{8,9},{9,10},{10,1... | collective-permute-start | bytes 98312 | tf_op jit(solution)/shard_map/ppermute | solution.py:140
  90.2 50.0 %collective-permute-start.3 = (f32[64,128]{1,0:T(8,128)S(1)}, f32[64,128]{1,0:T(8,128)}, u32[]{:S(2)}, u32[]{:S(2)}) collective-permute-start(f32[64,128]{1,0:T(8,128)S(1)} %get-tuple-element.36), channel_id=1, source_target_pairs={{1,0},{2,1},{3,2},{4,3},{5,4},{6,5},{7,6},{8,7},{9,8},{10,9},{11,1... | collective-permute-start | bytes 98312 | tf_op jit(solution)/shard_map/ppermute | solution.py:139
  97.3 12.5 %collective-permute-start.4 = (bf16[2,16,8,576]{3,2,0,1:T(8,128)(2,1)S(1)}, bf16[2,16,8,576]{3,2,0,1:T(8,128)(2,1)S(1)}, u32[]{:S(2)}, u32[]{:S(2)}) collective-permute-start(bf16[2,16,8,576]{3,2,0,1:T(8,128)(2,1)S(1)} %fusion.4), channel_id=1, source_target_pairs={{0,1},{1,0},{2,3},{3,2},{4,5},{5,4},{6,7},{7,6},{8,9},{9,8},{10,11... | collective-permute-start | bytes 884744 | tf_op jit(solution)/shard_map/ppermute | solution.py:40
  104.8 7.6 %collective-permute-start.7 = (bf16[16,8,128]{2,1,0:T(8,128)(2,1)S(1)}, bf16[16,8,128]{2,1,0:T(8,128)(2,1)S(1)}, u32[]{:S(2)}, u32[]{:S(2)}) collective-permute-start(bf16[16,8,128]{2,1,0:T(8,128)(2,1)S(1)} %fusion.28), channel_id=1, source_target_pairs={{0,2},{2,0},{1,3},{3,1},{4,6},{6,4},{5,7},{7,5},{8,10},{10,8},{9,1... | collective-permute-start | bytes 98312 | tf_op jit(solution)/shard_map/ppermute | solution.py:40
  109.9 28.0 %copy-start.2 = (bf16[8,512,128]{2,1,0:T(8,128)(2,1)S(1)}, bf16[8,512,128]{2,1,0:T(8,128)(2,1)}, u32[]{:S(2)}) copy-start(bf16[8,512,128]{2,1,0:T(8,128)(2,1)} %all_to_all.25) | copy-start | bytes 3145732
  110.0 9.9 %collective-permute-start.5 = (bf16[16,8,576]{2,1,0:T(8,128)(2,1)S(1)}, bf16[16,8,576]{2,1,0:T(8,128)(2,1)S(1)}, u32[]{:S(2)}, u32[]{:S(2)}) collective-permute-start(bf16[16,8,576]{2,1,0:T(8,128)(2,1)S(1)} %fusion.19), channel_id=1, source_target_pairs={{0,2},{2,0},{1,3},{3,1},{4,6},{6,4},{5,7},{7,5},{8,10},{10,8},{9,1... | collective-permute-start | bytes 442376 | tf_op jit(solution)/shard_map/ppermute | solution.py:40
  120.6 32.5 %all-to-all-start.4 = ((bf16[16,8,704]{2,1,0:T(8,128)(2,1)}), bf16[16,8,704]{2,1,0:T(8,128)(2,1)S(1)}, u32[]{:S(2)}, u32[]{:S(2)}) async-start(bf16[16,8,704]{2,1,0:T(8,128)(2,1)} %pad_maximum_fusion.2), calls=%async_computation.4 | async-start | bytes 393216 | tf_op jit(solution)/shard_map/all_to_all | solution.py:28
  153.3 18.7 %collective-permute-start.8 = (f32[8,128]{1,0:T(8,128)S(1)}, f32[8,128]{1,0:T(8,128)S(1)}, u32[]{:S(2)}, u32[]{:S(2)}) collective-permute-start(f32[8,128]{1,0:T(8,128)S(1)} %slice.139), channel_id=1, source_target_pairs={{0,0},{1,64},{2,128},{3,192},{4,256},{5,320},{6,384},{7,448},{8,1}... | collective-permute-start | bytes 12296 | tf_op jit(solution)/shard_map/ppermute | solution.py:163

commit v2 on v1

v2 whole, which is shorter than its diff:
```python
import math

import jax
import jax.numpy as jnp
from jax import lax
from jax.experimental import pallas as pl
from jax.experimental.pallas import tpu as pltpu
from jax.sharding import Mesh, PartitionSpec as P

TILE = ("z", "xh", "core")
BF16 = jnp.bfloat16
F32 = jnp.float32


def normal_cdf(value):
    return 0.5 * (1.0 + jax.scipy.special.erf(value / math.sqrt(2.0)))


def normal_pdf(value):
    return jnp.exp(-0.5 * value * value) / math.sqrt(2.0 * math.pi)


def dot(spec, left, right):
    return jnp.einsum(spec, left, right, preferred_element_type=F32)


def swap(block, axis):
    return lax.all_to_all(block, axis, 0, 0)


def spread(block):
    count = lax.axis_size("chan")
    return swap(jnp.broadcast_to(block[None], (count,) + block.shape), "chan")


def halved(block, axis, dim):
    mine = lax.axis_index(axis)
    keep = lax.dynamic_index_in_dim(block, mine, dim, keepdims=False)
    give = lax.dynamic_index_in_dim(block, 1 - mine, dim, keepdims=False).astype(BF16)
    return keep + lax.ppermute(give, axis, [(0, 1), (1, 0)]).astype(F32)


def mixed_kernel(mix_ref, hidden_ref, inner_ref, up_ref, down_ref):
    own_out, cells = inner_ref.shape
    n_cols = up_ref.shape[1]
    column = lax.rem(lax.broadcasted_iota(jnp.int32, (own_out, cells), 1), n_cols)
    lines = []
    for tap_row in range(3):
        first = 3 * own_out * tap_row
        heap = jnp.dot(
            mix_ref[first : first + 3 * own_out, :], hidden_ref[...], preferred_element_type=F32
        )
        left = pltpu.roll(heap[:own_out], 1, 1)
        right = pltpu.roll(heap[2 * own_out :], cells - 1, 1)
        lines.append(
            jnp.where(column > 0, left, 0.0)
            + heap[own_out : 2 * own_out]
            + jnp.where(column < n_cols - 1, right, 0.0)
        )
    inner_ref[...] = lines[1]
    inner_ref[:, n_cols:] += lines[0][:, : cells - n_cols]
    inner_ref[:, : cells - n_cols] += lines[2][:, n_cols:]
    down_ref[...] = lines[0][:, cells - n_cols :]
    up_ref[...] = lines[2][:, :n_cols]


def mixed_parts(mix, hidden, n_cols):
    cells = hidden.shape[1]
    own_out = mix.shape[0] // 9
    whole = pl.BlockSpec(memory_space=pltpu.VMEM)
    edge = jax.ShapeDtypeStruct((own_out, n_cols), F32)
    return pl.pallas_call(
        mixed_kernel,
        out_shape=(jax.ShapeDtypeStruct((own_out, cells), F32), edge, edge),
        in_specs=[whole, whole],
        out_specs=(whole, whole, whole),
        cost_estimate=pl.CostEstimate(
            flops=2 * mix.size * cells,
            bytes_accessed=2 * (mix.size + hidden.size) + 4 * own_out * cells,
            transcendentals=0,
        ),
        compiler_params=pltpu.CompilerParams(vmem_limit_bytes=32 << 20),
    )(mix, hidden)


def per_device(image, w_down, w_mix, cotangent):
    n_chan = lax.axis_size("chan")
    n_z, n_xh, n_core = (lax.axis_size(a) for a in TILE)
    n_tile = n_z * n_xh * n_core
    own_in, _, in_cols = image.shape
    own_out, n_rows, n_cols = cotangent.shape
    cells = n_rows * n_cols
    all_in = n_chan * own_in
    all_out = n_chan * own_out
    taps = 4 * own_in
    scale = 1.0 / math.sqrt(cells * n_tile)
    ahead = [(i, i + 1) for i in range(n_tile - 1)]
    back = [(i + 1, i) for i in range(n_tile - 1)]

    even_odd = (
        jnp.arange(in_cols)[:, None, None]
        == 2 * jnp.arange(n_cols)[None, None, :] + jnp.arange(2)[None, :, None]
    ).astype(BF16)
    own_patches = dot("crax,xbw->rabcw", image.reshape(own_in, n_rows, 2, in_cols), even_odd)
    own_patches = jnp.transpose(own_patches.astype(BF16), (1, 2, 3, 0, 4)).reshape(taps, cells)
    own_patches, cotangent = lax.optimization_barrier((own_patches, cotangent))
    patches = spread(own_patches)

    above = lax.ppermute(cotangent[:, n_rows - 1], TILE, ahead)
    below = lax.ppermute(cotangent[:, 0], TILE, back)
    rim = jnp.concatenate([above, cotangent.reshape(own_out, cells), below], axis=1)
    rim = rim.reshape(own_out, n_rows + 2, n_cols)
    rim = jnp.pad(rim, ((0, 0), (0, 0), (1, 1)))
    cols = jnp.concatenate(
        [
            rim[:, 2 - i : 2 - i + n_rows, 2 - j : 2 - j + n_cols].reshape(own_out, cells)
            for i in range(3)
            for j in range(3)
        ]
    )

    mix = jnp.transpose(w_mix, (0, 1, 3, 2)).reshape(9 * own_out, all_out)
    partial = dot("kc,kq->cq", mix, cols).astype(BF16).reshape(n_chan, own_out, cells)
    turned = w_down.reshape(2, 2, n_chan, own_in, own_out)
    turned = jnp.transpose(turned, (2, 4, 0, 1, 3)).reshape(n_chan, own_out, taps)
    spare = own_out * taps // cells
    turned = turned.reshape(n_chan, own_out // spare, spare, taps)
    turned = jnp.transpose(turned, (0, 2, 1, 3)).reshape(n_chan, spare, cells)
    partial = jnp.concatenate([partial, turned], axis=1)
    patches, partial = lax.optimization_barrier((patches, partial))
    partial = swap(partial, "chan")

    down = jnp.transpose(w_down.reshape(2, 2, n_chan, own_in, own_out), (4, 2, 0, 1, 3))
    down = down.reshape(own_out, 4 * all_in)
    patches = patches.reshape(4 * all_in, cells)
    preact = dot("dk,kq->dq", down, patches)
    cdf = normal_cdf(preact)
    hidden = (preact * cdf).astype(BF16)
    hidden, partial = lax.optimization_barrier((hidden, partial))
    hidden = spread(hidden).reshape(all_out, cells)

    grad_hidden = jnp.sum(partial[:, :own_out].astype(F32), axis=0)
    slope = cdf + preact * normal_pdf(preact)
    grad_pre = (grad_hidden * slope).astype(BF16)
    grad_down = dot("kq,dq->kd", patches, grad_pre)
    groups = n_tile // n_chan
    group = own_in // groups
    grad_down = grad_down.reshape(n_chan, 2, 2, groups, group, own_out)
    grad_down = jnp.transpose(grad_down, (0, 3, 2, 4, 1, 5)).reshape(n_tile, 2 * group, 2 * own_out)

    grad_pre, hidden = lax.optimization_barrier((grad_pre, hidden))
    all_pre = spread(grad_pre).reshape(all_out, cells)

    rows = all_out // n_tile
    grad_mix = dot("cq,kq->ck", hidden, cols).reshape(n_tile, rows, 9 * own_out)
    total = jnp.concatenate([grad_mix, grad_down], axis=-1)
    total = total.reshape(n_z, n_xh, n_core, rows, -1)
    total = halved(halved(total, "core", 2), "xh", 1).astype(BF16)
    total = jnp.sum(swap(total, "z").astype(F32), axis=0) * scale
    grad_mix = total[:, : 9 * own_out].reshape(rows, 3, 3, own_out)
    piece = total[:, 9 * own_out :].reshape(2, group, 2, own_out)
    grad_down = jnp.transpose(piece, (1, 2, 0, 3))

    inner, up, down_edge = mixed_parts(mix, hidden, n_cols)
    from_below = lax.ppermute(up, TILE, back)
    from_above = lax.ppermute(down_edge, TILE, ahead)
    edges = jnp.concatenate(
        [from_above, jnp.zeros((own_out, cells - 2 * n_cols), F32), from_below], axis=1
    )
    mixed = (inner + edges).astype(BF16).reshape(own_out, n_rows, n_cols)

    turned = partial[:, own_out:].reshape(n_chan, spare, own_out // spare, taps)
    turned = jnp.transpose(turned, (0, 2, 1, 3)).reshape(all_out, taps)
    grad_image = dot("dk,dq->kq", turned, all_pre).astype(BF16)
    grad_image = grad_image.reshape(2, 2, own_in, n_rows, n_cols)
    grad_image = dot("abcrw,xbw->crax", grad_image, even_odd)
    grad_image = grad_image.astype(BF16).reshape(image.shape)
    return (mixed, grad_mix, grad_down, grad_image)


def solution(mesh):
    grid = mesh.devices
    n_chan, n_tile = grid.shape
    split = Mesh(grid.reshape(n_chan, n_tile // 4, 2, 2), ("chan",) + TILE)
    return jax.shard_map(
        per_device,
        mesh=split,
        in_specs=(
            P("chan", TILE, None),
            P(None, None, None, "chan"),
            P(None, None, None, "chan"),
            P("chan", TILE, None),
        ),
        out_specs=(
            P("chan", TILE, None),
            P(TILE, None, None, "chan"),
            P(TILE, None, None, "chan"),
            P("chan", TILE, None),
        ),
        check_vma=False,
    )
```

time: 174 us -> 151 us (0.87)
  the two profiles are of different devices: /device:TPU:56 before, /device:TPU:103 now
where the time goes in v2:
time: 151 us; the launch traced here: 150 us
  waiting for transfers between devices  63.3 us (42%)
  starting transfers between devices  56.1 us (37%)
  local copies, waits for them, and re-layouts  14.9 us (10%)
  matrix products  8.21 us (5%)
  other arithmetic  5.29 us (4%)
    all_to_all x5, waiting for transfers between devices, swap(): return lax.all_to_all(block, axis, 0, 0)  43.7 us
    all_to_all x5, starting transfers between devices, swap(): return lax.all_to_all(block, axis, 0, 0)  31 us
    ppermute x2, waiting for transfers between devices, halved(): return keep + lax.ppermute(give, axis, [(0, 1), (1, 0)]).astype(F32)  12.7 us
    ppermute x1, starting transfers between devices, per_device(): from_above = lax.ppermute(down_edge, TILE, ahead)  8.5 us
    dot_general x7, matrix products, dot(): return jnp.einsum(spec, left, right, preferred_element_type=F32)  8.21 us
    ppermute x1, waiting for transfers between devices, per_device(): from_below = lax.ppermute(up, TILE, back)  6.94 us
    ppermute x2, starting transfers between devices, halved(): return keep + lax.ppermute(give, axis, [(0, 1), (1, 0)]).astype(F32)  6.65 us
    ppermute x1, starting transfers between devices, per_device(): above = lax.ppermute(cotangent[:, n_rows - 1], TILE, ahead)  6.16 us
  transfers between devices with their start and end apart: 11, of which 5 were waited for; matrix products, arithmetic and copies ran while one was open for 13% of the time, Pallas kernels for 1%

profile of v2, /device:TPU:103, one launch (start us, length us, event | category | flops | bytes accessed | tf_op | source)
XLA Modules:
  0.0 149.9 jit_solution(16578419465770685988)
XLA Ops:
  2.3 6.2 %collective-permute-start = (bf16[64,128]{1,0:T(8,128)(2,1)S(1)}, bf16[64,128]{1,0:T(8,128)(2,1)S(1)}, u32[]{:S(2)}, u32[]{:S(2)}) collective-permute-start(bf16[64,128]{1,0:T(8,128)(2,1)S(1)} %get-tuple-element.43), channel_id=1, source_target_pairs={{0,1},{1,2},{2,3},{3,4},{4,5},{5,6},{6,7},{7,8},{8,9},{9,10},{10,1... | collective-permute-start | bytes 49160 | tf_op jit(solution)/shard_map/ppermute | solution.py:109
  8.4 1.9 %collective-permute-start.1 = (bf16[64,128]{1,0:T(8,128)(2,1)S(1)}, bf16[64,128]{1,0:T(8,128)(2,1)S(1)}, u32[]{:S(2)}, u32[]{:S(2)}) collective-permute-start(bf16[64,128]{1,0:T(8,128)(2,1)S(1)} %get-tuple-element.44), channel_id=1, source_target_pairs={{1,0},{2,1},{3,2},{4,3},{5,4},{6,5},{7,6},{8,7},{9,8},{10,9},{11,1... | collective-permute-start | bytes 49160 | tf_op jit(solution)/shard_map/ppermute | solution.py:110
  10.4 1.6 %broadcast_in_dim.8 = bf16[8,128,1024]{2,1,0:T(8,128)(2,1)} broadcast(bf16[128,1024]{1,0:T(8,128)(2,1)S(1)} %bitcast.138), dimensions={1,2} | broadcast | bytes 2359296 | tf_op jit(solution)/shard_map/broadcast_in_dim | solution.py:33
  11.9 5.5 %all-to-all-start = ((bf16[8,128,1024]{2,1,0:T(8,128)(2,1)}), bf16[8,128,1024]{2,1,0:T(8,128)(2,1)}, u32[]{:S(2)}, u32[]{:S(2)}) async-start(bf16[8,128,1024]{2,1,0:T(8,128)(2,1)} %broadcast_in_dim.8), calls=%async_computation | async-start | bytes 4194304 | tf_op jit(solution)/shard_map/all_to_all | solution.py:28
  22.1 21.7 %all-to-all-done = bf16[8,128,1024]{2,1,0:T(8,128)(2,1)} async-done(((bf16[8,128,1024]{2,1,0:T(8,128)(2,1)}), bf16[8,128,1024]{2,1,0:T(8,128)(2,1)}, u32[]{:S(2)}, u32[]{:S(2)}) %all-to-all-start) | async-done | bytes 2097184 | tf_op jit(solution)/shard_map/all_to_all | solution.py:28
  43.8 4.4 %all-to-all-start.1 = ((bf16[8,72,1024]{2,1,0:T(8,128)(2,1)}), bf16[8,72,1024]{2,1,0:T(8,128)(2,1)S(1)}, u32[]{:S(2)}, u32[]{:S(2)}) async-start(bf16[8,72,1024]{2,1,0:T(8,128)(2,1)} %pad_maximum_fusion), calls=%async_computation.1 | async-start | bytes 2359296 | tf_op jit(solution)/shard_map/all_to_all | solution.py:28
  48.2 2.1 %multiply_convert_fusion = (bf16[64,1024]{1,0:T(8,128)(2,1)S(1)}, f32[64,1024]{1,0:T(8,128)S(1)}) fusion(bf16[1024,1024]{1,0:T(8,128)(2,1)} %bitcast.16, bf16[64,1024]{0,1:T(8,128)(2,1)S(1)} %bitcast.139), kind=kOutput, calls=%fused_computation.43 | convolution fusion | flops 134545408 | bytes 2621440 | tf_op jit(solution)/shard_map/dk,kq->dq/dot_general | solution.py:24
  50.4 13.4 %all-to-all-done.1 = bf16[8,72,1024]{2,1,0:T(8,128)(2,1)S(1)} async-done(((bf16[8,72,1024]{2,1,0:T(8,128)(2,1)}), bf16[8,72,1024]{2,1,0:T(8,128)(2,1)S(1)}, u32[]{:S(2)}, u32[]{:S(2)}) %all-to-all-start.1) | async-done | bytes 1179680 | tf_op jit(solution)/shard_map/all_to_all | solution.py:28
  63.8 1.2 broadcast_in_dim.9
  65.1 4.4 %all-to-all-start.2 = ((bf16[8,64,1024]{2,1,0:T(8,128)(2,1)}), bf16[8,64,1024]{2,1,0:T(8,128)(2,1)S(1)}, u32[]{:S(2)}, u32[]{:S(2)}) async-start(bf16[8,64,1024]{2,1,0:T(8,128)(2,1)} %broadcast_in_dim.9), calls=%async_computation.2 | async-start | bytes 2097152 | tf_op jit(solution)/shard_map/all_to_all | solution.py:28
  69.5 2.7 %copy.33 = bf16[8,128,1024]{2,0,1:T(8,128)(2,1)S(1)} copy(bf16[8,128,1024]{2,1,0:T(8,128)(2,1)} %all-to-all-done) | data formatting | bytes 4194304 | tf_op jit(solution)/shard_map/optimization_barrier | solution.py:130
  74.0 8.5 %all-to-all-done.2 = bf16[8,64,1024]{2,1,0:T(8,128)(2,1)S(1)} async-done(((bf16[8,64,1024]{2,1,0:T(8,128)(2,1)}), bf16[8,64,1024]{2,1,0:T(8,128)(2,1)S(1)}, u32[]{:S(2)}, u32[]{:S(2)}) %all-to-all-start.2) | async-done | bytes 1048608 | tf_op jit(solution)/shard_map/all_to_all | solution.py:28
  82.4 2.3 %fusion.28 = f32[512,576]{1,0:T(8,128)S(1)} fusion(bf16[512,1024]{1,0:T(8,128)(2,1)S(1)} %bitcast.128, bf16[576,1024]{1,0:T(8,128)(2,1)} %copy-done.5), kind=kOutput, calls=%fused_computation.69 | convolution fusion | flops 603979776 | bytes 3407872 | tf_op jit(solution)/shard_map/cq,kq->ck/dot_general | solution.py:24
  85.6 4.7 %collective-permute-start.4 = (bf16[16,2,8,704]{3,2,1,0:T(8,128)(2,1)}, bf16[16,2,8,704]{3,2,1,0:T(8,128)(2,1)}, u32[]{:S(2)}, u32[]{:S(2)}) collective-permute-start(bf16[16,2,8,704]{3,2,1,0:T(8,128)(2,1)} %fusion.9), channel_id=1, source_target_pairs={{0,1},{1,0},{2,3},{3,2},{4,5},{5,4},{6,7},{7,6},{8,9},{9,8},{10,11... | collective-permute-start | bytes 1081352 | tf_op jit(solution)/shard_map/ppermute | solution.py:40
  91.4 5.0 %all-to-all-start.4 = ((bf16[8,64,1024]{2,1,0:T(8,128)(2,1)}), bf16[8,64,1024]{2,1,0:T(8,128)(2,1)}, u32[]{:S(2)}, u32[]{:S(2)}) async-start(bf16[8,64,1024]{2,1,0:T(8,128)(2,1)} %broadcast_in_dim.11), calls=%async_computation.4 | async-start | bytes 2097152 | tf_op jit(solution)/shard_map/all_to_all | solution.py:28
  96.5 1.2 fusion.8
  98.5 1.9 %collective-permute-start.5 = (bf16[16,8,704]{2,1,0:T(8,128)(2,1)S(1)}, bf16[16,8,704]{2,1,0:T(8,128)(2,1)S(1)}, u32[]{:S(2)}, u32[]{:S(2)}) collective-permute-start(bf16[16,8,704]{2,1,0:T(8,128)(2,1)S(1)} %fusion.23), channel_id=1, source_target_pairs={{0,2},{2,0},{1,3},{3,1},{4,6},{6,4},{5,7},{7,5},{8,10},{10,8},{9,1... | collective-permute-start | bytes 540680 | tf_op jit(solution)/shard_map/ppermute | solution.py:40
  100.5 12.7 %collective-permute-done.5 = bf16[16,8,704]{2,1,0:T(8,128)(2,1)S(1)} collective-permute-done((bf16[16,8,704]{2,1,0:T(8,128)(2,1)S(1)}, bf16[16,8,704]{2,1,0:T(8,128)(2,1)S(1)}, u32[]{:S(2)}, u32[]{:S(2)}) %collective-permute-start.5) | collective-permute-done | bytes 180256 | tf_op jit(solution)/shard_map/ppermute | solution.py:40
  113.2 1.7 %fusion.10 = bf16[16,8,704]{2,1,0:T(8,128)(2,1)} fusion(bf16[16,8,704]{2,1,0:T(8,128)(2,1)S(1)} %collective-permute-done.5, f32[16,2,8,704]{3,2,1,0:T(8,128)} %copy-done.2, s32[]{:T(128)S(6)} %select_n.16), kind=kLoop, calls=%fused_computation.29 | loop fusion | flops 270336 | bytes 720900 | tf_op jit(solution)/shard_map/convert_element_type | solution.py:158
  114.9 11.6 %all-to-all-start.3 = ((bf16[16,8,704]{2,1,0:T(8,128)(2,1)}), bf16[16,8,704]{2,1,0:T(8,128)(2,1)S(1)}, u32[]{:S(2)}, u32[]{:S(2)}) async-start(bf16[16,8,704]{2,1,0:T(8,128)(2,1)} %fusion.10), calls=%async_computation.3 | async-start | bytes 393216 | tf_op jit(solution)/shard_map/all_to_all | solution.py:28
  127.4 8.5 %collective-permute-start.2 = (f32[64,128]{1,0:T(8,128)S(1)}, f32[64,128]{1,0:T(8,128)S(1)}, u32[]{:S(2)}, u32[]{:S(2)}) collective-permute-start(f32[64,128]{1,0:T(8,128)S(1)} %get-tuple-element.23), channel_id=1, source_target_pairs={{0,1},{1,2},{2,3},{3,4},{4,5},{5,6},{6,7},{7,8},{8,9},{9,10},{10,1... | collective-permute-start | bytes 98312 | tf_op jit(solution)/shard_map/ppermute | solution.py:166
  135.9 1.9 %collective-permute-start.3 = (f32[64,128]{1,0:T(8,128)S(1)}, f32[64,128]{1,0:T(8,128)S(1)}, u32[]{:S(2)}, u32[]{:S(2)}) collective-permute-start(f32[64,128]{1,0:T(8,128)S(1)} %get-tuple-element.24), channel_id=1, source_target_pairs={{1,0},{2,1},{3,2},{4,3},{5,4},{6,5},{7,6},{8,7},{9,8},{10,9},{11,1... | collective-permute-start | bytes 98312 | tf_op jit(solution)/shard_map/ppermute | solution.py:165
  137.9 6.9 %collective-permute-done.3 = f32[64,128]{1,0:T(8,128)S(1)} collective-permute-done((f32[64,128]{1,0:T(8,128)S(1)}, f32[64,128]{1,0:T(8,128)S(1)}, u32[]{:S(2)}, u32[]{:S(2)}) %collective-permute-start.3) | collective-permute-done | bytes 32800 | tf_op jit(solution)/shard_map/ppermute | solution.py:165
  145.6 1.6 %fusion.2 = bf16[16,8,8,128]{3,1,2,0:T(8,128)(2,1)S(1)} fusion(bf16[512,128]{1,0:T(8,128)(2,1)S(1)} %bitcast.135, bf16[512,1024]{1,0:T(8,128)(2,1)} %bitcast.35), kind=kOutput, calls=%fused_computation.14 | convolution fusion | flops 134348800 | bytes 1441792 | tf_op jit(solution)/shard_map/dk,dq->kq/dot_general | solution.py:24
  (72 shorter events, 15.0 us)
Async XLA Ops:
  0.6 1.6 %copy-start.3 = (bf16[64,8,128]{2,1,0:T(8,128)(2,1)S(1)}, bf16[64,8,128]{2,1,0:T(8,128)(2,1)}, u32[]{:S(2)}) copy-start(bf16[64,8,128]{2,1,0:T(8,128)(2,1)} %param.7) | copy-start | bytes 393220
  2.3 16.1 %collective-permute-start = (bf16[64,128]{1,0:T(8,128)(2,1)S(1)}, bf16[64,128]{1,0:T(8,128)(2,1)S(1)}, u32[]{:S(2)}, u32[]{:S(2)}) collective-permute-start(bf16[64,128]{1,0:T(8,128)(2,1)S(1)} %get-tuple-element.43), channel_id=1, source_target_pairs={{0,1},{1,2},{2,3},{3,4},{4,5},{5,6},{6,7},{7,8},{8,9},{9,10},{10,1... | collective-permute-start | bytes 49160 | tf_op jit(solution)/shard_map/ppermute | solution.py:109
  8.4 9.9 %collective-permute-start.1 = (bf16[64,128]{1,0:T(8,128)(2,1)S(1)}, bf16[64,128]{1,0:T(8,128)(2,1)S(1)}, u32[]{:S(2)}, u32[]{:S(2)}) collective-permute-start(bf16[64,128]{1,0:T(8,128)(2,1)S(1)} %get-tuple-element.44), channel_id=1, source_target_pairs={{1,0},{2,1},{3,2},{4,3},{5,4},{6,5},{7,6},{8,7},{9,8},{10,9},{11,1... | collective-permute-start | bytes 49160 | tf_op jit(solution)/shard_map/ppermute | solution.py:110
  11.9 5.5 %copy-start.4 = (bf16[2,2,256,64]{2,3,1,0:T(8,128)(2,1)S(1)}, bf16[2,2,256,64]{2,3,1,0:T(8,128)(2,1)}, u32[]{:S(2)}) copy-start(bf16[2,2,256,64]{2,3,1,0:T(8,128)(2,1)} %param.5) | copy-start | bytes 393220
  11.9 31.9 %all-to-all-start = ((bf16[8,128,1024]{2,1,0:T(8,128)(2,1)}), bf16[8,128,1024]{2,1,0:T(8,128)(2,1)}, u32[]{:S(2)}, u32[]{:S(2)}) async-start(bf16[8,128,1024]{2,1,0:T(8,128)(2,1)} %broadcast_in_dim.8), calls=%async_computation | async-start | bytes 4194304 | tf_op jit(solution)/shard_map/all_to_all | solution.py:28
  18.8 1.1 copy-start
  19.1 1.9 %copy-start.5 = (bf16[576,1024]{1,0:T(8,128)(2,1)}, bf16[576,1024]{1,0:T(8,128)(2,1)S(1)}, u32[]{:S(2)}) copy-start(bf16[576,1024]{1,0:T(8,128)(2,1)S(1)} %bitcast_dynamic-update-slice_fusion) | copy-start | bytes 3538948
  43.8 20.0 %all-to-all-start.1 = ((bf16[8,72,1024]{2,1,0:T(8,128)(2,1)}), bf16[8,72,1024]{2,1,0:T(8,128)(2,1)S(1)}, u32[]{:S(2)}, u32[]{:S(2)}) async-start(bf16[8,72,1024]{2,1,0:T(8,128)(2,1)} %pad_maximum_fusion), calls=%async_computation.1 | async-start | bytes 2359296 | tf_op jit(solution)/shard_map/all_to_all | solution.py:28
  63.8 8.4 %copy-start.1 = (bf16[8,72,1024]{2,1,0:T(8,128)(2,1)}, bf16[8,72,1024]{2,1,0:T(8,128)(2,1)S(1)}, u32[]{:S(2)}) copy-start(bf16[8,72,1024]{2,1,0:T(8,128)(2,1)S(1)} %all-to-all-done.1) | copy-start | bytes 3538948
  65.1 17.4 %all-to-all-start.2 = ((bf16[8,64,1024]{2,1,0:T(8,128)(2,1)}), bf16[8,64,1024]{2,1,0:T(8,128)(2,1)S(1)}, u32[]{:S(2)}, u32[]{:S(2)}) async-start(bf16[8,64,1024]{2,1,0:T(8,128)(2,1)} %broadcast_in_dim.9), calls=%async_computation.2 | async-start | bytes 2097152 | tf_op jit(solution)/shard_map/all_to_all | solution.py:28
  85.6 10.9 %collective-permute-start.4 = (bf16[16,2,8,704]{3,2,1,0:T(8,128)(2,1)}, bf16[16,2,8,704]{3,2,1,0:T(8,128)(2,1)}, u32[]{:S(2)}, u32[]{:S(2)}) collective-permute-start(bf16[16,2,8,704]{3,2,1,0:T(8,128)(2,1)} %fusion.9), channel_id=1, source_target_pairs={{0,1},{1,0},{2,3},{3,2},{4,5},{5,4},{6,7},{7,6},{8,9},{9,8},{10,11... | collective-permute-start | bytes 1081352 | tf_op jit(solution)/shard_map/ppermute | solution.py:40
  91.4 23.4 %all-to-all-start.4 = ((bf16[8,64,1024]{2,1,0:T(8,128)(2,1)}), bf16[8,64,1024]{2,1,0:T(8,128)(2,1)}, u32[]{:S(2)}, u32[]{:S(2)}) async-start(bf16[8,64,1024]{2,1,0:T(8,128)(2,1)} %broadcast_in_dim.11), calls=%async_computation.4 | async-start | bytes 2097152 | tf_op jit(solution)/shard_map/all_to_all | solution.py:28
  97.6 0.9 copy-start.2
  98.5 14.6 %collective-permute-start.5 = (bf16[16,8,704]{2,1,0:T(8,128)(2,1)S(1)}, bf16[16,8,704]{2,1,0:T(8,128)(2,1)S(1)}, u32[]{:S(2)}, u32[]{:S(2)}) collective-permute-start(bf16[16,8,704]{2,1,0:T(8,128)(2,1)S(1)} %fusion.23), channel_id=1, source_target_pairs={{0,2},{2,0},{1,3},{3,1},{4,6},{6,4},{5,7},{7,5},{8,10},{10,8},{9,1... | collective-permute-start | bytes 540680 | tf_op jit(solution)/shard_map/ppermute | solution.py:40
  114.9 33.4 %all-to-all-start.3 = ((bf16[16,8,704]{2,1,0:T(8,128)(2,1)}), bf16[16,8,704]{2,1,0:T(8,128)(2,1)S(1)}, u32[]{:S(2)}, u32[]{:S(2)}) async-start(bf16[16,8,704]{2,1,0:T(8,128)(2,1)} %fusion.10), calls=%async_computation.3 | async-start | bytes 393216 | tf_op jit(solution)/shard_map/all_to_all | solution.py:28
  126.5 19.0 %slice-start = ((bf16[8,72,1024]{2,1,0:T(8,128)(2,1)}), bf16[8,8,1024]{2,1,0:T(8,128)(2,1)S(1)}, s32[]{:S(2)}) async-start(bf16[8,72,1024]{2,1,0:T(8,128)(2,1)} %copy-done.1), calls=%async_computation.5 | async-start | bytes 262144 | tf_op jit(solution)/shard_map/slice | solution.py:172
  127.4 10.5 %collective-permute-start.2 = (f32[64,128]{1,0:T(8,128)S(1)}, f32[64,128]{1,0:T(8,128)S(1)}, u32[]{:S(2)}, u32[]{:S(2)}) collective-permute-start(f32[64,128]{1,0:T(8,128)S(1)} %get-tuple-element.23), channel_id=1, source_target_pairs={{0,1},{1,2},{2,3},{3,4},{4,5},{5,6},{6,7},{7,8},{8,9},{9,10},{10,1... | collective-permute-start | bytes 98312 | tf_op jit(solution)/shard_map/ppermute | solution.py:166
  135.9 8.9 %collective-permute-start.3 = (f32[64,128]{1,0:T(8,128)S(1)}, f32[64,128]{1,0:T(8,128)S(1)}, u32[]{:S(2)}, u32[]{:S(2)}) collective-permute-start(f32[64,128]{1,0:T(8,128)S(1)} %get-tuple-element.24), channel_id=1, source_target_pairs={{1,0},{2,1},{3,2},{4,3},{5,4},{6,5},{7,6},{8,7},{9,8},{10,9},{11,1... | collective-permute-start | bytes 98312 | tf_op jit(solution)/shard_map/ppermute | solution.py:165

commit v3 on v2

v3 whole, which is shorter than its diff:
```python
import math

import jax
import jax.numpy as jnp
from jax import lax
from jax.experimental import pallas as pl
from jax.experimental.pallas import tpu as pltpu
from jax.sharding import Mesh, PartitionSpec as P

CHAN = ("y", "xl")
TILE = ("z", "xh", "core")
BF16 = jnp.bfloat16
F32 = jnp.float32


def normal_cdf(value):
    return 0.5 * (1.0 + jax.scipy.special.erf(value / math.sqrt(2.0)))


def normal_pdf(value):
    return jnp.exp(-0.5 * value * value) / math.sqrt(2.0 * math.pi)


def dot(spec, left, right):
    return jnp.einsum(spec, left, right, preferred_element_type=F32)


def swap(block, axis):
    return lax.all_to_all(block, axis, 0, 0)


def halved(block, axis, dim):
    mine = lax.axis_index(axis)
    keep = lax.dynamic_index_in_dim(block, mine, dim, keepdims=False)
    give = lax.dynamic_index_in_dim(block, 1 - mine, dim, keepdims=False).astype(BF16)
    return keep + lax.ppermute(give, axis, [(0, 1), (1, 0)]).astype(F32)


def call(kernel, outs, flops, *args):
    whole = pl.BlockSpec(memory_space=pltpu.VMEM)
    moved = sum(a.size * a.dtype.itemsize for a in args + tuple(outs))
    return pl.pallas_call(
        kernel,
        out_shape=tuple(outs),
        in_specs=[whole] * len(args),
        out_specs=(whole,) * len(outs),
        cost_estimate=pl.CostEstimate(flops=flops, bytes_accessed=moved, transcendentals=0),
        compiler_params=pltpu.CompilerParams(vmem_limit_bytes=12 << 20),
    )(*args)


def shape(dims, dtype):
    return jax.ShapeDtypeStruct(dims, dtype)


def moved(block, step, n_cols):
    width = block.shape[1]
    column = lax.rem(lax.broadcasted_iota(jnp.int32, block.shape, 1), n_cols)
    if step > 0:
        return jnp.where(column > 0, pltpu.roll(block, 1, 1), 0.0)
    return jnp.where(column < n_cols - 1, pltpu.roll(block, width - 1, 1), 0.0)


def grad_hidden_kernel(
    above_hbm, cot_hbm, below_hbm, mix_hbm, turned_hbm, cols_ref, out_hbm, rim_ref, mix_ref,
    part_ref, sems,
):
    own_out, n_cols = above_hbm.shape
    cells = cot_hbm.shape[1]
    n_chan, pair_out, half = part_ref.shape
    n_half = cells // half
    ins = [
        pltpu.make_async_copy(above_hbm, rim_ref.at[:, pl.ds(0, n_cols)], sems.at[0]),
        pltpu.make_async_copy(cot_hbm, rim_ref.at[:, pl.ds(n_cols, cells)], sems.at[1]),
        pltpu.make_async_copy(below_hbm, rim_ref.at[:, pl.ds(n_cols + cells, n_cols)], sems.at[2]),
    ]
    filters = pltpu.make_async_copy(mix_hbm, mix_ref, sems.at[3])
    outs = [
        pltpu.make_async_copy(
            turned_hbm.at[k],
            out_hbm.at[k, pl.ds(pair_out, turned_hbm.shape[1])],
            sems.at[4 + k],
        )
        for k in range(n_chan)
    ]
    for copy in ins + [filters] + outs:
        copy.start()
    for copy in ins:
        copy.wait()
    rim = rim_ref[...]
    wide = rim.astype(F32)
    taps = [moved(wide, -1, n_cols).astype(BF16), rim, moved(wide, 1, n_cols).astype(BF16)]
    for i in range(3):
        for j in range(3):
            first = (3 * i + j) * own_out
            start = (2 - i) * n_cols
            cols_ref[first : first + own_out, :] = taps[j][:, start : start + cells]
    filters.wait()
    for y in range(n_chan // n_half):
        part = lax.dot_general(
            mix_ref[:, y * pair_out : (y + 1) * pair_out],
            cols_ref[...],
            (((0,), (0,)), ((), ())),
            preferred_element_type=F32,
        ).astype(BF16)
        for h in range(n_half):
            k = y * n_half + h
            part_ref[k] = part[:, h * half : (h + 1) * half]
            copy = pltpu.make_async_copy(
                part_ref.at[k], out_hbm.at[k, pl.ds(0, pair_out)], sems.at[4 + n_chan + k]
            )
            copy.start()
            outs.append(copy)
    for copy in outs:
        copy.wait()


VM = pl.BlockSpec(memory_space=pltpu.VMEM)
FAR = pl.BlockSpec(memory_space=pl.ANY)
HBM = pl.BlockSpec(memory_space=pltpu.HBM)
SM = pl.BlockSpec(memory_space=pltpu.SMEM)


def run(kernel, in_specs, out_specs, outs, scratch, flops, *args):
    size = sum(a.size * a.dtype.itemsize for a in args + tuple(outs))
    return pl.pallas_call(
        kernel,
        out_shape=tuple(outs),
        in_specs=in_specs,
        out_specs=tuple(out_specs),
        scratch_shapes=scratch,
        cost_estimate=pl.CostEstimate(flops=flops, bytes_accessed=size, transcendentals=0),
        compiler_params=pltpu.CompilerParams(vmem_limit_bytes=16 << 20),
    )(*args)


def grad_hidden_parts(above, cot, below, mix, turned):
    n_chan, spare, half = turned.shape
    own_out, cells = cot.shape
    n_cols = above.shape[1]
    pair_out = mix.shape[1] * cells // (n_chan * half)
    return run(
        grad_hidden_kernel,
        [FAR, FAR, FAR, HBM, HBM],
        [VM, HBM],
        (
            shape((9 * own_out, cells), BF16),
            shape((n_chan, pair_out + spare, half), BF16),
        ),
        [
            pltpu.VMEM((own_out, cells + 2 * n_cols), BF16),
            pltpu.VMEM(mix.shape, BF16),
            pltpu.VMEM((n_chan, pair_out, half), BF16),
            pltpu.SemaphoreType.DMA((2 * n_chan + 4,)),
        ],
        2 * mix.size * cells,
        above,
        cot,
        below,
        mix,
        turned,
    )


def spread_kernel(hidden_ref, halo_ref, out_ref):
    n_chan, all_rows, half = out_ref.shape
    pair_out, n_cols = halo_ref.shape
    spare = all_rows - pair_out
    halo = jnp.concatenate(
        [halo_ref[q * spare : (q + 1) * spare, :] for q in range(half // n_cols)], axis=1
    )
    for k in range(n_chan):
        out_ref[k, :pair_out, :] = hidden_ref[...]
        out_ref[k, pair_out:, :] = halo


def grad_pre_kernel(side_ref, got_ref, slope_ref, patches_ref, pre_ref, keep_ref, give_ref):
    n_chan = got_ref.shape[0]
    pair_out = slope_ref.shape[0]
    own_out = pair_out // 2
    taps = patches_ref.shape[0] // n_chan
    total = got_ref[0, :pair_out, :].astype(F32)
    for k in range(1, n_chan):
        total += got_ref[k, :pair_out, :].astype(F32)
    pre = (total * slope_ref[...]).astype(BF16)
    pre_ref[...] = pre
    first = side_ref[0] == 0
    rows = taps // 2
    for k in range(n_chan):
        down = lax.dot_general(
            patches_ref[k * taps : (k + 1) * taps, :],
            pre,
            (((1,), (1,)), ((), ())),
            preferred_element_type=F32,
        )
        sides = [
            jnp.concatenate(
                [down[:rows, h * own_out : (h + 1) * own_out],
                 down[rows:, h * own_out : (h + 1) * own_out]],
                axis=1,
            )
            for h in range(2)
        ]
        keep_ref[k * rows : (k + 1) * rows, :] = jnp.where(first, sides[0], sides[1])
        give_ref[k * rows : (k + 1) * rows, :] = jnp.where(first, sides[1], sides[0]).astype(BF16)


def spread_parts(hidden, halo, n_chan):
    rows = hidden.shape[0] + halo.size // hidden.shape[1]
    (out,) = run(
        spread_kernel,
        [VM, VM],
        [VM],
        (shape((n_chan, rows, hidden.shape[1]), BF16),),
        [],
        0,
        hidden,
        halo,
    )
    return out


def grad_pre_parts(side, got, slope, patches):
    pair_out = slope.shape[0]
    down = (patches.shape[0] // 2, pair_out)
    return run(
        grad_pre_kernel,
        [SM, VM, VM, VM],
        [VM, VM, VM],
        (shape(slope.shape, BF16), shape(down, F32), shape(down, BF16)),
        [],
        2 * patches.size * pair_out,
        side,
        got,
        slope,
        patches,
    )


def grad_mix_kernel(
    core_ref, both_hbm, cols_ref, down_hbm, more_hbm, keep_ref, give_hbm, hidden_ref, down_ref,
    more_ref, give_ref, sems,
):
    n_group, rows, width = keep_ref.shape
    n_chan, _, half = both_hbm.shape
    all_out, cells = hidden_ref.shape
    taps = cols_ref.shape[0]
    n_half = cells // half
    pair_out = all_out * n_half // n_chan
    maps = []
    for k in range(n_chan):
        y, h = divmod(k, n_half)
        maps.append(
            pltpu.make_async_copy(
                both_hbm.at[k, pl.ds(0, pair_out)],
                hidden_ref.at[pl.ds(y * pair_out, pair_out), pl.ds(h * half, half)],
                sems.at[k],
            )
        )
    downs = [
        pltpu.make_async_copy(down_hbm, down_ref, sems.at[n_chan]),
        pltpu.make_async_copy(more_hbm, more_ref, sems.at[n_chan + 1]),
    ]
    for copy in maps + downs:
        copy.start()
    first = core_ref[0] == 0
    for copy in downs:
        copy.wait()
    parts = 2
    size = all_out // parts
    step = n_group // parts
    blank = jnp.zeros((size, width - taps - down_ref.shape[1]), F32)
    for part in range(parts):
        for copy in maps[part * n_chan // parts : (part + 1) * n_chan // parts]:
            copy.wait()
        at = slice(part * size, (part + 1) * size)
        total = lax.dot_general(
            hidden_ref[at, :],
            cols_ref[...],
            (((1,), (1,)), ((), ())),
            preferred_element_type=F32,
        )
        extra = down_ref[at, :] + more_ref[at, :].astype(F32)
        total = jnp.concatenate([total, extra, blank], axis=1)
        total = total.reshape(step, 2, rows, width)
        to = slice(part * step, (part + 1) * step)
        keep_ref[to] = jnp.where(first, total[:, 0], total[:, 1])
        give_ref[to] = jnp.where(first, total[:, 1], total[:, 0]).astype(BF16)
    give = pltpu.make_async_copy(give_ref, give_hbm, sems.at[n_chan + 2])
    give.start()
    give.wait()


def grad_mix_parts(core, both, cols, down, more, n_tile, width):
    n_chan, _, half = both.shape
    all_out = down.shape[0]
    rows = all_out // n_tile
    return run(
        grad_mix_kernel,
        [SM, HBM, VM, FAR, FAR],
        [VM, FAR],
        (shape((n_tile // 2, rows, width), F32), shape((n_tile // 2, rows, width), BF16)),
        [
            pltpu.VMEM((all_out, cols.shape[1]), BF16),
            pltpu.VMEM(down.shape, F32),
            pltpu.VMEM(down.shape, BF16),
            pltpu.VMEM((n_tile // 2, rows, width), BF16),
            pltpu.SemaphoreType.DMA((n_chan + 3,)),
        ],
        2 * all_out * cols.size,
        core,
        both,
        cols,
        down,
        more,
    )


def mixed_kernel(mix_ref, both_ref, out_ref):
    own_out, cells = out_ref.shape
    n_chan, all_rows, half = both_ref.shape
    n_half = cells // half
    n_y = n_chan // n_half
    pair_out = mix_ref.shape[1] // n_y
    spare = all_rows - pair_out
    n_cols = spare * half // pair_out

    def edge(k):
        return jnp.concatenate(
            [both_ref[k, pair_out:, q * n_cols : (q + 1) * n_cols] for q in range(half // n_cols)]
        )

    hidden = jnp.concatenate(
        [
            jnp.concatenate(
                [edge(y * n_half + n_half - 1)]
                + [both_ref[y * n_half + h, :pair_out, :] for h in range(n_half)]
                + [edge(y * n_half)],
                axis=1,
            )
            for y in range(n_y)
        ]
    )
    total = jnp.zeros((3 * own_out, cells), F32)
    for i in range(3):
        total += jnp.dot(
            mix_ref[3 * own_out * i : 3 * own_out * (i + 1), :],
            hidden[:, i * n_cols : i * n_cols + cells],
            preferred_element_type=F32,
        )
    out_ref[...] = (
        moved(total[:own_out], 1, n_cols)
        + total[own_out : 2 * own_out]
        + moved(total[2 * own_out :], -1, n_cols)
    ).astype(BF16)


def per_device(image, w_down, w_mix, cotangent):
    n_y, n_xl = (lax.axis_size(a) for a in CHAN)
    n_z, n_xh, n_core = (lax.axis_size(a) for a in TILE)
    n_chan = n_y * n_xl
    n_tile = n_z * n_xh * n_core
    own_in, _, in_cols = image.shape
    own_out, n_rows, n_cols = cotangent.shape
    cells = n_rows * n_cols
    half = cells // n_xl
    pair_out = n_xl * own_out
    all_in = n_chan * own_in
    all_out = n_chan * own_out
    taps = 4 * own_in
    groups = n_tile // n_chan
    group = own_in // groups
    scale = 1.0 / math.sqrt(cells * n_tile)
    ahead = [(i, i + 1) for i in range(n_tile - 1)]
    back = [(i + 1, i) for i in range(n_tile - 1)]
    flip = [(0, 1), (1, 0)]
    side = lax.axis_index("xl")
    first = side == 0

    above = lax.ppermute(cotangent[:, n_rows - 1], TILE, ahead)
    below = lax.ppermute(cotangent[:, 0], TILE, back)

    even_odd = (
        jnp.arange(in_cols)[:, None, None]
        == 2 * jnp.arange(n_cols)[None, None, :] + jnp.arange(2)[None, :, None]
    ).astype(BF16)
    sent = dot("crax,xbw->rabcw", image.reshape(own_in, n_rows, 2, in_cols), even_odd)
    sent = sent.astype(BF16).reshape(n_xl, n_rows // n_xl, 2, 2, groups, group, n_cols)
    sent = jnp.transpose(sent, (0, 2, 4, 3, 5, 1, 6)).reshape(n_xl, taps, half)
    sent = jnp.broadcast_to(sent[None], (n_y,) + sent.shape).reshape(n_chan, taps, half)
    patches = swap(sent, CHAN)

    mix = jnp.transpose(w_mix, (0, 1, 3, 2)).reshape(9 * own_out, all_out)
    turned = jnp.transpose(w_down.reshape(2, 2, n_y, n_xl, own_in, own_out), (2, 5, 3, 0, 1, 4))
    wide = n_xl * taps
    spare = own_out * wide // half
    turned = turned.reshape(n_y, own_out // spare, spare, wide)
    turned = jnp.transpose(turned, (0, 2, 1, 3)).reshape(n_y, 1, spare, half)
    turned = jnp.broadcast_to(turned, (n_y, n_xl, spare, half)).reshape(n_chan, spare, half)
    other_down = lax.ppermute(w_down, "xl", flip)
    cols, partial = grad_hidden_parts(
        above,
        cotangent.reshape(own_out, cells),
        below,
        mix,
        turned,
    )
    patches, partial, other_down = lax.optimization_barrier((patches, partial, other_down))
    partial = swap(partial, CHAN)

    down = jnp.stack([jnp.where(first, w_down, other_down), jnp.where(first, other_down, w_down)])
    down = down.reshape(n_xl, 2, 2, n_chan, groups, group, own_out)
    down = jnp.transpose(down, (0, 6, 3, 1, 4, 2, 5)).reshape(pair_out, 4 * all_in)
    patches = patches.reshape(4 * all_in, half)
    preact = dot("dk,kq->dq", down, patches)
    cdf = normal_cdf(preact)
    slope = cdf + preact * normal_pdf(preact)
    hidden = (preact * cdf).astype(BF16)
    halo = jnp.where(first, hidden[:, :n_cols], hidden[:, half - n_cols :])
    halo = lax.ppermute(halo, ("xl",) + TILE, back + [(n_tile + i, n_tile + j) for i, j in ahead])
    both = spread_parts(hidden, halo, n_chan)
    both, slope, partial = lax.optimization_barrier((both, slope, partial))
    both = swap(both, CHAN)
    grad_pre, down_keep, down_give = grad_pre_parts(side.reshape(1), partial, slope, patches)
    down_more = lax.ppermute(down_give, "xl", flip)
    all_pre = jnp.broadcast_to(grad_pre[None], (n_y,) + grad_pre.shape)
    both, down_more, all_pre = lax.optimization_barrier((both, down_more, all_pre))
    all_pre = swap(all_pre, "y")

    rows = all_out // n_tile
    width = 12 * own_out
    core = lax.axis_index("core").reshape(1)
    keep, give = grad_mix_parts(core, both, cols, down_keep, down_more, n_tile, width)
    total = keep + lax.ppermute(give, "core", flip).astype(F32)
    total, all_pre = lax.optimization_barrier((total.astype(BF16), all_pre))
    total = swap(total, ("z", "xh"))
    total = jnp.sum(total.astype(F32), axis=0) * scale
    grad_mix = total[:, : 9 * own_out].reshape(rows, 3, 3, own_out)
    piece = total[:, 9 * own_out : 11 * own_out].reshape(2, group, 2, own_out)
    grad_down = jnp.transpose(piece, (1, 2, 0, 3))

    (mixed,) = call(
        mixed_kernel, (shape((own_out, cells), BF16),), 2 * mix.size * cells, mix, both
    )
    mixed = mixed.reshape(own_out, n_rows, n_cols)

    turned = partial[:, pair_out:].reshape(n_chan, spare, own_out // spare, wide)
    turned = jnp.transpose(turned, (0, 2, 1, 3)).reshape(n_y, pair_out, wide)
    grad_image = dot("ydk,ydq->kq", turned, all_pre)
    grad_image = grad_image.astype(BF16).reshape(n_xl, taps, half)
    mine = jnp.where(first, grad_image[0], grad_image[1])
    theirs = lax.ppermute(jnp.where(first, grad_image[1], grad_image[0]), "xl", flip)
    grad_image = jnp.concatenate(
        [jnp.where(first, mine, theirs), jnp.where(first, theirs, mine)], axis=1
    )
    grad_image = grad_image.reshape(2, 2, own_in, n_rows, n_cols)
    grad_image = dot("abcrw,xbw->crax", grad_image, even_odd)
    grad_image = grad_image.astype(BF16).reshape(image.shape)
    return (mixed, grad_mix, grad_down, grad_image)


def solution(mesh):
    grid = mesh.devices
    n_chan, n_tile = grid.shape
    split = Mesh(grid.reshape(n_chan // 2, 2, n_tile // 4, 2, 2), CHAN + TILE)
    return jax.shard_map(
        per_device,
        mesh=split,
        in_specs=(
            P(CHAN, TILE, None),
            P(None, None, None, CHAN),
            P(None, None, None, CHAN),
            P(CHAN, TILE, None),
        ),
        out_specs=(
            P(CHAN, TILE, None),
            P(TILE, None, None, CHAN),
            P(TILE, None, None, CHAN),
            P(CHAN, TILE, None),
        ),
        check_vma=False,
    )
```

time: 151 us -> 147 us (0.974)
  the two profiles are of different devices: /device:TPU:103 before, /device:TPU:4 now
where the time goes in v3:
time: 147 us; the launch traced here: 146 us
  starting transfers between devices  62.6 us (43%)
  waiting for transfers between devices  48.6 us (33%)
  local copies, waits for them, and re-layouts  17.6 us (12%)
  Pallas kernels  10.8 us (7%)
  matrix products  2.91 us (2%)
  other arithmetic  2.48 us (2%)
    all_to_all x5, starting transfers between devices, swap(): return lax.all_to_all(block, axis, 0, 0)  39.1 us
    all_to_all x5, waiting for transfers between devices, swap(): return lax.all_to_all(block, axis, 0, 0)  31 us
    ppermute x1, waiting for transfers between devices, per_device(): down_more = lax.ppermute(down_give, 'xl', flip)  9.1 us
    pallas_call x4, Pallas kernels, run(): pl.pallas_call(kernel, out_shape=tuple(outs), in_specs=in_specs, out_spec...  8.56 us
    unnamed x31, local copies, waits for them, and re-layouts  8.42 us
    ppermute x1, starting transfers between devices, per_device(): below = lax.ppermute(cotangent[:, 0], TILE, back)  5.15 us
    ppermute x1, starting transfers between devices, per_device(): lax.ppermute(halo, ('xl',) + TILE, back + [(n_tile + i, n_tile + j) for i...  4.44 us
    ppermute x1, starting transfers between devices, per_device(): other_down = lax.ppermute(w_down, 'xl', flip)  4.06 us
  transfers between devices with their start and end apart: 12, of which 9 were waited for; matrix products, arithmetic and copies ran while one was open for 8% of the time, Pallas kernels for 5%

profile of v3, /device:TPU:4, one launch (start us, length us, event | category | flops | bytes accessed | tf_op | source)
XLA Modules:
  0.0 146.0 jit_solution(7343362074764750048)
XLA Ops:
  3.5 5.2 %all-to-all-start = ((bf16[8,128,512]{2,1,0:T(8,128)(2,1)}), bf16[8,128,512]{2,1,0:T(8,128)(2,1)S(1)}, u32[]{:S(2)}, u32[]{:S(2)}) async-start(bf16[8,128,512]{2,1,0:T(8,128)(2,1)} %bitcast.9), calls=%async_computation | async-start | bytes 2097152 | tf_op jit(solution)/shard_map/all_to_all | solution.py:29
  8.9 4.1 %collective-permute-start.2 = (bf16[2,2,256,64]{3,2,1,0:T(8,128)(2,1)S(1)}, bf16[2,2,256,64]{3,2,1,0:T(8,128)(2,1)}, u32[]{:S(2)}, u32[]{:S(2)}) collective-permute-start(bf16[2,2,256,64]{3,2,1,0:T(8,128)(2,1)S(1)} %copy.37), channel_id=1, source_target_pairs={{0,64},{64,0},{1,65},{65,1},{2,66},{66,2},{3,67},{67,3},{4,68},{68... | collective-permute-start | bytes 393224 | tf_op jit(solution)/shard_map/ppermute | solution.py:400
  13.1 1.9 %collective-permute-start = (bf16[64,128]{1,0:T(8,128)(2,1)S(1)}, bf16[64,128]{1,0:T(8,128)(2,1)S(1)}, u32[]{:S(2)}, u32[]{:S(2)}) collective-permute-start(bf16[64,128]{1,0:T(8,128)(2,1)S(1)} %bitcast.103), channel_id=1, source_target_pairs={{0,1},{1,2},{2,3},{3,4},{4,5},{5,6},{6,7},{7,8},{8,9},{9,10},{10,1... | collective-permute-start | bytes 49160 | tf_op jit(solution)/shard_map/ppermute | solution.py:380
  15.0 5.1 %collective-permute-start.1 = (bf16[64,128]{1,0:T(8,128)(2,1)S(1)}, bf16[64,128]{1,0:T(8,128)(2,1)S(1)}, u32[]{:S(2)}, u32[]{:S(2)}) collective-permute-start(bf16[64,128]{1,0:T(8,128)(2,1)S(1)} %bitcast.104), channel_id=1, source_target_pairs={{1,0},{2,1},{3,2},{4,3},{5,4},{6,5},{7,6},{8,7},{9,8},{10,9},{11,1... | collective-permute-start | bytes 49160 | tf_op jit(solution)/shard_map/ppermute | solution.py:381
  22.7 3.2 %collective-permute-done.1.below_hbm = bf16[64,128]{1,0:T(8,128)(2,1)S(1)} collective-permute-done((bf16[64,128]{1,0:T(8,128)(2,1)S(1)}, bf16[64,128]{1,0:T(8,128)(2,1)S(1)}, u32[]{:S(2)}, u32[]{:S(2)}) %collective-permute-start.1) | collective-permute-done | bytes 16416 | tf_op jit(solution)/shard_map/ppermute | solution.py:381
  26.0 3.8 %shard_map.75 = (bf16[576,1024]{1,0:T(8,128)(2,1)S(1)}, bf16[8,160,512]{2,1,0:T(8,128)(2,1)S(1)}) custom-call(bf16[64,128]{1,0:T(8,128)(2,1)S(1)} %collective-permute-done.above_hbm, bf16[64,1024]{1,0:T(8,128)(2,1)S(1)} %bitcast.84, bf16[64,128]{1,0:T(8,128)(2,1)S(1)} %collective-permute-done.1.below_hbm, bf16[576,512]{1,0:T(8,128)(2,1)S(1)} %bitcast.86, ...), custom_call_target="tpu_custom_call" | custom-call | flops 603979776 | bytes 3506176 | tf_op jit(solution)/shard_map/pallas_call | solution.py:126
  30.9 5.4 %all-to-all-start.1 = ((bf16[8,160,512]{2,1,0:T(8,128)(2,1)}), bf16[8,160,512]{2,1,0:T(8,128)(2,1)S(1)}, u32[]{:S(2)}, u32[]{:S(2)}) async-start(bf16[8,160,512]{2,1,0:T(8,128)(2,1)} %copy-done.1), calls=%async_computation.1 | async-start | bytes 2621440 | tf_op jit(solution)/shard_map/all_to_all | solution.py:29
  39.4 2.0 %reshape.116 = bf16[128,1024]{0,1:T(8,128)(2,1)} reshape(bf16[2,64,8,2,8,2,4]{1,0,6,5,4,3,2:T(2,128)(2,1)} %copy.39) | data formatting | bytes 524288 | tf_op jit(solution)/shard_map/reshape | solution.py:413
  41.4 2.1 %fusion.6 = (f32[128,512]{1,0:T(8,128)}, bf16[128,512]{1,0:T(8,128)(2,1)S(1)}) fusion(bf16[128,1024]{0,1:T(8,128)(2,1)} %reshape.116, bf16[1024,512]{1,0:T(8,128)(2,1)S(1)} %bitcast.81), kind=kOutput, calls=%fused_computation.13 | convolution fusion | flops 134873088 | bytes 1703936 | tf_op jit(solution)/shard_map/dk,kq->dq/dot_general | solution.py:25
  43.5 4.4 %collective-permute-start.3 = (bf16[128,128]{1,0:T(8,128)(2,1)S(1)}, bf16[128,128]{1,0:T(8,128)(2,1)S(1)}, u32[]{:S(2)}, u32[]{:S(2)}) collective-permute-start(bf16[128,128]{1,0:T(8,128)(2,1)S(1)} %slice_select_fusion), channel_id=1, source_target_pairs={{1,0},{2,1},{3,2},{4,3},{5,4},{6,5},{7,6},{8,7},{9,8},{10,9},{11,1... | collective-permute-start | bytes 98312 | tf_op jit(solution)/shard_map/ppermute | solution.py:420
  50.7 2.6 %all-to-all-done.1.got_ref = bf16[8,160,512]{2,1,0:T(8,128)(2,1)S(1)} async-done(((bf16[8,160,512]{2,1,0:T(8,128)(2,1)}), bf16[8,160,512]{2,1,0:T(8,128)(2,1)S(1)}, u32[]{:S(2)}, u32[]{:S(2)}) %all-to-all-start.1) | async-done | bytes 1310752 | tf_op jit(solution)/shard_map/all_to_all | solution.py:29
  53.3 4.9 %all-to-all-start.2 = ((bf16[8,160,512]{2,1,0:T(8,128)(2,1)}), bf16[8,160,512]{2,1,0:T(8,128)(2,1)}, u32[]{:S(2)}, u32[]{:S(2)}) async-start(bf16[8,160,512]{2,1,0:T(8,128)(2,1)} %copy-done), calls=%async_computation.2 | async-start | bytes 2621440 | tf_op jit(solution)/shard_map/all_to_all | solution.py:29
  61.8 3.9 %collective-permute-start.4 = (bf16[512,128]{1,0:T(8,128)(2,1)}, bf16[512,128]{1,0:T(8,128)(2,1)S(1)}, u32[]{:S(2)}, u32[]{:S(2)}) collective-permute-start(bf16[512,128]{1,0:T(8,128)(2,1)} %get-tuple-element.29), channel_id=1, source_target_pairs={{0,64},{64,0},{1,65},{65,1},{2,66},{66,2},{3,67},{67,3},{4,68},{68... | collective-permute-start | bytes 393224 | tf_op jit(solution)/shard_map/ppermute | solution.py:425
  65.7 9.1 %collective-permute-done.4.more_hbm = bf16[512,128]{1,0:T(8,128)(2,1)S(1)} collective-permute-done((bf16[512,128]{1,0:T(8,128)(2,1)}, bf16[512,128]{1,0:T(8,128)(2,1)S(1)}, u32[]{:S(2)}, u32[]{:S(2)}) %collective-permute-start.4) | collective-permute-done | bytes 131104 | tf_op jit(solution)/shard_map/ppermute | solution.py:425
  75.4 1.8 %broadcast_in_dim.27 = bf16[4,128,512]{2,1,0:T(8,128)(2,1)} broadcast(bf16[128,512]{1,0:T(8,128)(2,1)} %copy-done.5), dimensions={1,2} | broadcast | bytes 655360 | tf_op jit(solution)/shard_map/broadcast_in_dim | solution.py:426
  78.1 3.4 %shard_map.79 = (f32[32,8,768]{2,1,0:T(8,128)S(1)}, bf16[32,8,768]{2,1,0:T(8,128)(2,1)}) custom-call(s32[1]{0:T(128)} %bitcast.22.core_ref, bf16[8,160,512]{2,1,0:T(8,128)(2,1)} %all-to-all-done.2.both_ref.both_hbm, bf16[576,1024]{1,0:T(8,128)(2,1)S(1)} %get-tuple-element.32.cols_ref, f32[512,128]{1,0:T(8,128)S(1)} %copy-done.4, ...), custom_call_target="tpu_custom_call" | custom-call | flops 603979776 | bytes 4063236 | tf_op jit(solution)/shard_map/pallas_call | solution.py:126
  81.5 1.9 %collective-permute-start.5 = (bf16[32,8,768]{2,1,0:T(8,128)(2,1)}, bf16[32,8,768]{2,1,0:T(8,128)(2,1)S(1)}, u32[]{:S(2)}, u32[]{:S(2)}) collective-permute-start(bf16[32,8,768]{2,1,0:T(8,128)(2,1)} %get-tuple-element.36), channel_id=1, source_target_pairs={{0,1},{1,0},{2,3},{3,2},{4,5},{5,4},{6,7},{7,6},{8,9},{9,8},{10,11... | collective-permute-start | bytes 1179656 | tf_op jit(solution)/shard_map/ppermute | solution.py:434
  83.5 3.5 %all-to-all-start.3 = ((bf16[4,128,512]{2,1,0:T(8,128)(2,1)}), bf16[4,128,512]{2,1,0:T(8,128)(2,1)S(1)}, u32[]{:S(2)}, u32[]{:S(2)}) async-start(bf16[4,128,512]{2,1,0:T(8,128)(2,1)} %broadcast_in_dim.27), calls=%async_computation.3 | async-start | bytes 1048576 | tf_op jit(solution)/shard_map/all_to_all | solution.py:29
  87.8 9.6 %all-to-all-done.3 = bf16[4,128,512]{2,1,0:T(8,128)(2,1)S(1)} async-done(((bf16[4,128,512]{2,1,0:T(8,128)(2,1)}), bf16[4,128,512]{2,1,0:T(8,128)(2,1)S(1)}, u32[]{:S(2)}, u32[]{:S(2)}) %all-to-all-start.3) | async-done | bytes 524320 | tf_op jit(solution)/shard_map/all_to_all | solution.py:29
  97.3 20.1 %all-to-all-start.4 = ((bf16[32,8,768]{2,1,0:T(8,128)(2,1)}), bf16[32,8,768]{2,1,0:T(8,128)(2,1)S(1)}, u32[]{:S(2)}, u32[]{:S(2)}) async-start(bf16[32,8,768]{2,1,0:T(8,128)(2,1)} %add_convert_fusion), calls=%async_computation.4 | async-start | bytes 786432 | tf_op jit(solution)/shard_map/all_to_all | solution.py:29
  117.8 2.2 %collective-permute-start.6 = (bf16[128,512]{1,0:T(8,128)(2,1)S(1)}, bf16[128,512]{1,0:T(8,128)(2,1)S(1)}, u32[]{:S(2)}, u32[]{:S(2)}) collective-permute-start(bf16[128,512]{1,0:T(8,128)(2,1)S(1)} %broadcast_select_fusion.4), channel_id=1, source_target_pairs={{0,64},{64,0},{1,65},{65,1},{2,66},{66,2},{3,67},{67,3},{4,68},{68... | collective-permute-start | bytes 393224 | tf_op jit(solution)/shard_map/ppermute | solution.py:452
  120.1 2.2 %shard_map.78 = bf16[64,1024]{1,0:T(8,128)(2,1)S(1)} custom-call(bf16[576,512]{1,0:T(8,128)(2,1)S(1)} %bitcast.87, bf16[8,160,512]{2,1,0:T(8,128)(2,1)} %all-to-all-done.2.both_ref.both_hbm), custom_call_target="tpu_custom_call" | custom-call | flops 603979776 | bytes 2031616 | tf_op jit(solution)/shard_map/pallas_call | solution.py:42
  122.9 2.0 %collective-permute-done.6 = bf16[128,512]{1,0:T(8,128)(2,1)S(1)} collective-permute-done((bf16[128,512]{1,0:T(8,128)(2,1)S(1)}, bf16[128,512]{1,0:T(8,128)(2,1)S(1)}, u32[]{:S(2)}, u32[]{:S(2)}) %collective-permute-start.6) | collective-permute-done | bytes 131104 | tf_op jit(solution)/shard_map/ppermute | solution.py:452
  126.2 18.2 %all-to-all-done.4 = bf16[32,8,768]{2,1,0:T(8,128)(2,1)S(1)} async-done(((bf16[32,8,768]{2,1,0:T(8,128)(2,1)}), bf16[32,8,768]{2,1,0:T(8,128)(2,1)S(1)}, u32[]{:S(2)}, u32[]{:S(2)}) %all-to-all-start.4) | async-done | bytes 393248 | tf_op jit(solution)/shard_map/all_to_all | solution.py:29
  (70 shorter events, 22.3 us)
Async XLA Ops:
  3.5 5.2 %copy-start.10 = (bf16[2,2,256,64]{2,3,1,0:T(8,128)(2,1)S(1)}, bf16[2,2,256,64]{2,3,1,0:T(8,128)(2,1)}, u32[]{:S(2)}) copy-start(bf16[2,2,256,64]{2,3,1,0:T(8,128)(2,1)} %param.5) | copy-start | bytes 393220
  3.5 9.5 %copy-start.9 = (bf16[64,8,128]{2,1,0:T(8,128)(2,1)S(1)}, bf16[64,8,128]{2,1,0:T(8,128)(2,1)}, u32[]{:S(2)}) copy-start(bf16[64,8,128]{2,1,0:T(8,128)(2,1)} %param.7) | copy-start | bytes 393220
  3.5 27.4 %all-to-all-start = ((bf16[8,128,512]{2,1,0:T(8,128)(2,1)}), bf16[8,128,512]{2,1,0:T(8,128)(2,1)S(1)}, u32[]{:S(2)}, u32[]{:S(2)}) async-start(bf16[8,128,512]{2,1,0:T(8,128)(2,1)} %bitcast.9), calls=%async_computation | async-start | bytes 2097152 | tf_op jit(solution)/shard_map/all_to_all | solution.py:29
  8.9 20.9 %copy-start.8 = (bf16[2,2,256,64]{3,2,1,0:T(8,128)(2,1)}, bf16[2,2,256,64]{3,2,1,0:T(8,128)(2,1)S(1)}, u32[]{:S(2)}) copy-start(bf16[2,2,256,64]{3,2,1,0:T(8,128)(2,1)S(1)} %copy.37) | copy-start | bytes 393220
  8.9 17.1 %copy-start.6 = (bf16[3,3,512,64]{2,3,1,0:T(8,128)(2,1)S(1)}, bf16[3,3,512,64]{2,3,1,0:T(8,128)(2,1)}, u32[]{:S(2)}) copy-start(bf16[3,3,512,64]{2,3,1,0:T(8,128)(2,1)} %param.6) | copy-start | bytes 1769476
  8.9 21.9 %collective-permute-start.2 = (bf16[2,2,256,64]{3,2,1,0:T(8,128)(2,1)S(1)}, bf16[2,2,256,64]{3,2,1,0:T(8,128)(2,1)}, u32[]{:S(2)}, u32[]{:S(2)}) collective-permute-start(bf16[2,2,256,64]{3,2,1,0:T(8,128)(2,1)S(1)} %copy.37), channel_id=1, source_target_pairs={{0,64},{64,0},{1,65},{65,1},{2,66},{66,2},{3,67},{67,3},{4,68},{68... | collective-permute-start | bytes 393224 | tf_op jit(solution)/shard_map/ppermute | solution.py:400
  13.1 9.7 %collective-permute-start = (bf16[64,128]{1,0:T(8,128)(2,1)S(1)}, bf16[64,128]{1,0:T(8,128)(2,1)S(1)}, u32[]{:S(2)}, u32[]{:S(2)}) collective-permute-start(bf16[64,128]{1,0:T(8,128)(2,1)S(1)} %bitcast.103), channel_id=1, source_target_pairs={{0,1},{1,2},{2,3},{3,4},{4,5},{5,6},{6,7},{7,8},{8,9},{9,10},{10,1... | collective-permute-start | bytes 49160 | tf_op jit(solution)/shard_map/ppermute | solution.py:380
  15.0 10.9 %collective-permute-start.1 = (bf16[64,128]{1,0:T(8,128)(2,1)S(1)}, bf16[64,128]{1,0:T(8,128)(2,1)S(1)}, u32[]{:S(2)}, u32[]{:S(2)}) collective-permute-start(bf16[64,128]{1,0:T(8,128)(2,1)S(1)} %bitcast.104), channel_id=1, source_target_pairs={{1,0},{2,1},{3,2},{4,3},{5,4},{6,5},{7,6},{8,7},{9,8},{10,9},{11,1... | collective-permute-start | bytes 49160 | tf_op jit(solution)/shard_map/ppermute | solution.py:381
  29.8 1.1 copy-start.1
  30.9 22.5 %all-to-all-start.1 = ((bf16[8,160,512]{2,1,0:T(8,128)(2,1)}), bf16[8,160,512]{2,1,0:T(8,128)(2,1)S(1)}, u32[]{:S(2)}, u32[]{:S(2)}) async-start(bf16[8,160,512]{2,1,0:T(8,128)(2,1)} %copy-done.1), calls=%async_computation.1 | async-start | bytes 2621440 | tf_op jit(solution)/shard_map/all_to_all | solution.py:29
  43.5 6.0 %collective-permute-start.3 = (bf16[128,128]{1,0:T(8,128)(2,1)S(1)}, bf16[128,128]{1,0:T(8,128)(2,1)S(1)}, u32[]{:S(2)}, u32[]{:S(2)}) collective-permute-start(bf16[128,128]{1,0:T(8,128)(2,1)S(1)} %slice_select_fusion), channel_id=1, source_target_pairs={{1,0},{2,1},{3,2},{4,3},{5,4},{6,5},{7,6},{8,7},{9,8},{10,9},{11,1... | collective-permute-start | bytes 98312 | tf_op jit(solution)/shard_map/ppermute | solution.py:420
  49.6 1.1 copy-start
  53.3 22.1 %all-to-all-start.2 = ((bf16[8,160,512]{2,1,0:T(8,128)(2,1)}), bf16[8,160,512]{2,1,0:T(8,128)(2,1)}, u32[]{:S(2)}, u32[]{:S(2)}) async-start(bf16[8,160,512]{2,1,0:T(8,128)(2,1)} %copy-done), calls=%async_computation.2 | async-start | bytes 2621440 | tf_op jit(solution)/shard_map/all_to_all | solution.py:29
  58.2 0.9 copy-start.2
  60.4 0.7 copy-start.3
  61.1 0.6 copy-start.5
  61.8 13.0 %collective-permute-start.4 = (bf16[512,128]{1,0:T(8,128)(2,1)}, bf16[512,128]{1,0:T(8,128)(2,1)S(1)}, u32[]{:S(2)}, u32[]{:S(2)}) collective-permute-start(bf16[512,128]{1,0:T(8,128)(2,1)} %get-tuple-element.29), channel_id=1, source_target_pairs={{0,64},{64,0},{1,65},{65,1},{2,66},{66,2},{3,67},{67,3},{4,68},{68... | collective-permute-start | bytes 393224 | tf_op jit(solution)/shard_map/ppermute | solution.py:425
  77.2 0.9 copy-start.4
  81.5 5.4 %collective-permute-start.5 = (bf16[32,8,768]{2,1,0:T(8,128)(2,1)}, bf16[32,8,768]{2,1,0:T(8,128)(2,1)S(1)}, u32[]{:S(2)}, u32[]{:S(2)}) collective-permute-start(bf16[32,8,768]{2,1,0:T(8,128)(2,1)} %get-tuple-element.36), channel_id=1, source_target_pairs={{0,1},{1,0},{2,3},{3,2},{4,5},{5,4},{6,7},{7,6},{8,9},{9,8},{10,11... | collective-permute-start | bytes 1179656 | tf_op jit(solution)/shard_map/ppermute | solution.py:434
  83.5 13.9 %all-to-all-start.3 = ((bf16[4,128,512]{2,1,0:T(8,128)(2,1)}), bf16[4,128,512]{2,1,0:T(8,128)(2,1)S(1)}, u32[]{:S(2)}, u32[]{:S(2)}) async-start(bf16[4,128,512]{2,1,0:T(8,128)(2,1)} %broadcast_in_dim.27), calls=%async_computation.3 | async-start | bytes 1048576 | tf_op jit(solution)/shard_map/all_to_all | solution.py:29
  97.3 47.1 %all-to-all-start.4 = ((bf16[32,8,768]{2,1,0:T(8,128)(2,1)}), bf16[32,8,768]{2,1,0:T(8,128)(2,1)S(1)}, u32[]{:S(2)}, u32[]{:S(2)}) async-start(bf16[32,8,768]{2,1,0:T(8,128)(2,1)} %add_convert_fusion), calls=%async_computation.4 | async-start | bytes 786432 | tf_op jit(solution)/shard_map/all_to_all | solution.py:29
  117.4 2.6 %copy-start.7 = (bf16[3,3,512,64]{2,3,1,0:T(8,128)(2,1)S(1)}, bf16[3,3,512,64]{2,3,1,0:T(8,128)(2,1)}, u32[]{:S(2)}) copy-start(bf16[3,3,512,64]{2,3,1,0:T(8,128)(2,1)} %param.6) | copy-start | bytes 1769476
  117.8 7.1 %collective-permute-start.6 = (bf16[128,512]{1,0:T(8,128)(2,1)S(1)}, bf16[128,512]{1,0:T(8,128)(2,1)S(1)}, u32[]{:S(2)}, u32[]{:S(2)}) collective-permute-start(bf16[128,512]{1,0:T(8,128)(2,1)S(1)} %broadcast_select_fusion.4), channel_id=1, source_target_pairs={{0,64},{64,0},{1,65},{65,1},{2,66},{66,2},{3,67},{67,3},{4,68},{68... | collective-permute-start | bytes 393224 | tf_op jit(solution)/shard_map/ppermute | solution.py:452

commit v4 on v3

v4 whole, which is shorter than its diff:
```python
import math

import jax
import jax.numpy as jnp
from jax import lax
from jax.experimental import pallas as pl
from jax.experimental.pallas import tpu as pltpu
from jax.sharding import Mesh, PartitionSpec as P

CHAN = ("y", "xl")
TILE = ("z", "xh", "core")
BF16 = jnp.bfloat16
F32 = jnp.float32


def normal_cdf(value):
    return 0.5 * (1.0 + jax.scipy.special.erf(value / math.sqrt(2.0)))


def normal_pdf(value):
    return jnp.exp(-0.5 * value * value) / math.sqrt(2.0 * math.pi)


def dot(spec, left, right):
    return jnp.einsum(spec, left, right, preferred_element_type=F32)


def swap(block, axis):
    return lax.all_to_all(block, axis, 0, 0)


def halved(block, axis, dim):
    mine = lax.axis_index(axis)
    keep = lax.dynamic_index_in_dim(block, mine, dim, keepdims=False)
    give = lax.dynamic_index_in_dim(block, 1 - mine, dim, keepdims=False).astype(BF16)
    return keep + lax.ppermute(give, axis, [(0, 1), (1, 0)]).astype(F32)


def call(kernel, outs, flops, *args):
    whole = pl.BlockSpec(memory_space=pltpu.VMEM)
    moved = sum(a.size * a.dtype.itemsize for a in args + tuple(outs))
    return pl.pallas_call(
        kernel,
        out_shape=tuple(outs),
        in_specs=[whole] * len(args),
        out_specs=(whole,) * len(outs),
        cost_estimate=pl.CostEstimate(flops=flops, bytes_accessed=moved, transcendentals=0),
        compiler_params=pltpu.CompilerParams(vmem_limit_bytes=12 << 20),
    )(*args)


def call_core(kernel, outs, flops, core, *args):
    whole = pl.BlockSpec(memory_space=pltpu.VMEM)
    moved = sum(a.size * a.dtype.itemsize for a in args + tuple(outs))
    return pl.pallas_call(
        kernel,
        out_shape=tuple(outs),
        in_specs=[pl.BlockSpec(memory_space=pltpu.SMEM)] + [whole] * len(args),
        out_specs=(whole,) * len(outs),
        cost_estimate=pl.CostEstimate(flops=flops, bytes_accessed=moved, transcendentals=0),
        compiler_params=pltpu.CompilerParams(vmem_limit_bytes=12 << 20),
    )(core, *args)


def shape(dims, dtype):
    return jax.ShapeDtypeStruct(dims, dtype)


def moved(block, step, n_cols):
    width = block.shape[1]
    column = lax.rem(lax.broadcasted_iota(jnp.int32, block.shape, 1), n_cols)
    if step > 0:
        return jnp.where(column > 0, pltpu.roll(block, 1, 1), 0.0)
    return jnp.where(column < n_cols - 1, pltpu.roll(block, width - 1, 1), 0.0)


def grad_hidden_kernel(above_ref, cot_ref, below_ref, mix_ref, turned_ref, cols_ref, out_ref):
    own_out, n_cols = above_ref.shape
    cells = cot_ref.shape[1]
    n_chan, spare, half = turned_ref.shape
    pair_out = out_ref.shape[1] - spare
    n_half = cells // half
    rim = jnp.concatenate([above_ref[...], cot_ref[...], below_ref[...]], axis=1)
    wide = rim.astype(F32)
    taps = [moved(wide, -1, n_cols).astype(BF16), rim, moved(wide, 1, n_cols).astype(BF16)]
    for i in range(3):
        for j in range(3):
            first = (3 * i + j) * own_out
            start = (2 - i) * n_cols
            cols_ref[first : first + own_out, :] = taps[j][:, start : start + cells]
    for y in range(n_chan // n_half):
        part = lax.dot_general(
            mix_ref[:, y * pair_out : (y + 1) * pair_out],
            cols_ref[...],
            (((0,), (0,)), ((), ())),
            preferred_element_type=F32,
        ).astype(BF16)
        for h in range(n_half):
            out_ref[y * n_half + h, :pair_out, :] = part[:, h * half : (h + 1) * half]
            out_ref[y * n_half + h, pair_out:, :] = turned_ref[y * n_half + h]


def spread_kernel(hidden_ref, halo_ref, out_ref):
    n_chan, all_rows, half = out_ref.shape
    pair_out, n_cols = halo_ref.shape
    spare = all_rows - pair_out
    halo = jnp.concatenate(
        [halo_ref[q * spare : (q + 1) * spare, :] for q in range(half // n_cols)], axis=1
    )
    for k in range(n_chan):
        out_ref[k, :pair_out, :] = hidden_ref[...]
        out_ref[k, pair_out:, :] = halo


def grad_pre_kernel(side_ref, got_ref, slope_ref, patches_ref, pre_ref, keep_ref, give_ref):
    n_chan = got_ref.shape[0]
    pair_out = slope_ref.shape[0]
    own_out = pair_out // 2
    taps = patches_ref.shape[0] // n_chan
    total = got_ref[0, :pair_out, :].astype(F32)
    for k in range(1, n_chan):
        total += got_ref[k, :pair_out, :].astype(F32)
    pre = (total * slope_ref[...]).astype(BF16)
    pre_ref[...] = pre
    first = side_ref[0] == 0
    rows = taps // 2
    for k in range(n_chan):
        down = lax.dot_general(
            patches_ref[k * taps : (k + 1) * taps, :],
            pre,
            (((1,), (1,)), ((), ())),
            preferred_element_type=F32,
        )
        sides = [
            jnp.concatenate(
                [down[:rows, h * own_out : (h + 1) * own_out],
                 down[rows:, h * own_out : (h + 1) * own_out]],
                axis=1,
            )
            for h in range(2)
        ]
        keep_ref[k * rows : (k + 1) * rows, :] = jnp.where(first, sides[0], sides[1])
        give_ref[k * rows : (k + 1) * rows, :] = jnp.where(first, sides[1], sides[0]).astype(BF16)


def grad_mix_kernel(core_ref, both_ref, cols_ref, down_ref, more_ref, keep_ref, give_ref):
    n_group, rows, width = keep_ref.shape
    n_chan, _, half = both_ref.shape
    taps, cells = cols_ref.shape
    n_half = cells // half
    pair_out = n_group * 2 * rows * n_half // n_chan
    first = core_ref[0] == 0
    step = pair_out // (2 * rows)
    blank = jnp.zeros((pair_out, width - taps - down_ref.shape[1]), F32)
    for y in range(n_chan // n_half):
        hidden = jnp.concatenate(
            [both_ref[y * n_half + h, :pair_out, :] for h in range(n_half)], axis=1
        )
        total = lax.dot_general(
            hidden, cols_ref[...], (((1,), (1,)), ((), ())), preferred_element_type=F32
        )
        at = slice(y * pair_out, (y + 1) * pair_out)
        extra = down_ref[at, :] + more_ref[at, :].astype(F32)
        total = jnp.concatenate([total, extra, blank], axis=1)
        total = total.reshape(step, 2, rows, width)
        keep_ref[y * step : (y + 1) * step] = jnp.where(first, total[:, 0], total[:, 1])
        give_ref[y * step : (y + 1) * step] = jnp.where(first, total[:, 1], total[:, 0]).astype(
            BF16
        )


def mixed_kernel(mix_ref, both_ref, out_ref):
    own_out, cells = out_ref.shape
    n_chan, all_rows, half = both_ref.shape
    n_half = cells // half
    n_y = n_chan // n_half
    pair_out = mix_ref.shape[1] // n_y
    spare = all_rows - pair_out
    n_cols = spare * half // pair_out

    def edge(k):
        return jnp.concatenate(
            [both_ref[k, pair_out:, q * n_cols : (q + 1) * n_cols] for q in range(half // n_cols)]
        )

    hidden = jnp.concatenate(
        [
            jnp.concatenate(
                [edge(y * n_half + n_half - 1)]
                + [both_ref[y * n_half + h, :pair_out, :] for h in range(n_half)]
                + [edge(y * n_half)],
                axis=1,
            )
            for y in range(n_y)
        ]
    )
    total = jnp.zeros((3 * own_out, cells), F32)
    for i in range(3):
        total += jnp.dot(
            mix_ref[3 * own_out * i : 3 * own_out * (i + 1), :],
            hidden[:, i * n_cols : i * n_cols + cells],
            preferred_element_type=F32,
        )
    out_ref[...] = (
        moved(total[:own_out], 1, n_cols)
        + total[own_out : 2 * own_out]
        + moved(total[2 * own_out :], -1, n_cols)
    ).astype(BF16)


def per_device(image, w_down, w_mix, cotangent):
    n_y, n_xl = (lax.axis_size(a) for a in CHAN)
    n_z, n_xh, n_core = (lax.axis_size(a) for a in TILE)
    n_chan = n_y * n_xl
    n_tile = n_z * n_xh * n_core
    own_in, _, in_cols = image.shape
    own_out, n_rows, n_cols = cotangent.shape
    cells = n_rows * n_cols
    half = cells // n_xl
    pair_out = n_xl * own_out
    all_in = n_chan * own_in
    all_out = n_chan * own_out
    taps = 4 * own_in
    groups = n_tile // n_chan
    group = own_in // groups
    scale = 1.0 / math.sqrt(cells * n_tile)
    ahead = [(i, i + 1) for i in range(n_tile - 1)]
    back = [(i + 1, i) for i in range(n_tile - 1)]
    flip = [(0, 1), (1, 0)]
    side = lax.axis_index("xl")
    first = side == 0

    other_down = lax.ppermute(w_down, "xl", flip)

    even_odd = (
        jnp.arange(in_cols)[:, None, None]
        == 2 * jnp.arange(n_cols)[None, None, :] + jnp.arange(2)[None, :, None]
    ).astype(BF16)
    sent = dot("crax,xbw->rabcw", image.reshape(own_in, n_rows, 2, in_cols), even_odd)
    sent = sent.astype(BF16).reshape(n_xl, n_rows // n_xl, 2, 2, groups, group, n_cols)
    sent = jnp.transpose(sent, (0, 2, 4, 3, 5, 1, 6)).reshape(n_xl, taps, half)
    sent = jnp.broadcast_to(sent[None], (n_y,) + sent.shape).reshape(n_chan, taps, half)
    sent, cotangent = lax.optimization_barrier((sent, cotangent))
    patches = swap(sent, CHAN)

    above = lax.ppermute(cotangent[:, n_rows - 1], TILE, ahead)
    below = lax.ppermute(cotangent[:, 0], TILE, back)

    mix = jnp.transpose(w_mix, (0, 1, 3, 2)).reshape(9 * own_out, all_out)
    turned = jnp.transpose(w_down.reshape(2, 2, n_y, n_xl, own_in, own_out), (2, 5, 3, 0, 1, 4))
    wide = n_xl * taps
    spare = own_out * wide // half
    turned = turned.reshape(n_y, own_out // spare, spare, wide)
    turned = jnp.transpose(turned, (0, 2, 1, 3)).reshape(n_y, 1, spare, half)
    turned = jnp.broadcast_to(turned, (n_y, n_xl, spare, half)).reshape(n_chan, spare, half)
    cols, partial = call(
        grad_hidden_kernel,
        (
            shape((9 * own_out, cells), BF16),
            shape((n_chan, pair_out + spare, half), BF16),
        ),
        2 * mix.size * cells,
        above,
        cotangent.reshape(own_out, cells),
        below,
        mix,
        turned,
    )
    patches, partial, other_down = lax.optimization_barrier((patches, partial, other_down))
    partial = swap(partial, CHAN)

    down = jnp.stack([jnp.where(first, w_down, other_down), jnp.where(first, other_down, w_down)])
    down = down.reshape(n_xl, 2, 2, n_chan, groups, group, own_out)
    down = jnp.transpose(down, (0, 6, 3, 1, 4, 2, 5)).reshape(pair_out, 4 * all_in)
    patches = patches.reshape(4 * all_in, half)
    preact = dot("dk,kq->dq", down, patches)
    cdf = normal_cdf(preact)
    slope = cdf + preact * normal_pdf(preact)
    hidden = (preact * cdf).astype(BF16)
    halo = jnp.where(first, hidden[:, :n_cols], hidden[:, half - n_cols :])
    halo = lax.ppermute(halo, ("xl",) + TILE, back + [(n_tile + i, n_tile + j) for i, j in ahead])
    (both,) = call(
        spread_kernel,
        (shape((n_chan, pair_out + pair_out * n_cols // half, half), BF16),),
        0,
        hidden,
        halo,
    )
    both, slope, partial = lax.optimization_barrier((both, slope, partial))
    both = swap(both, CHAN)
    grad_pre, down_keep, down_give = call_core(
        grad_pre_kernel,
        (
            shape((pair_out, half), BF16),
            shape((all_out, 2 * own_out), F32),
            shape((all_out, 2 * own_out), BF16),
        ),
        2 * patches.size * pair_out,
        side.reshape(1),
        partial,
        slope,
        patches,
    )
    down_more = lax.ppermute(down_give, "xl", flip)
    near = [grad_pre] + [
        lax.ppermute(grad_pre, "y", [(i, (i + k) % n_y) for i in range(n_y)])
        for k in range(1, n_y)
    ]

    rows = all_out // n_tile
    width = 12 * own_out
    keep, give = call_core(
        grad_mix_kernel,
        (
            shape((n_z * n_xh, rows, width), F32),
            shape((n_z * n_xh, rows, width), BF16),
        ),
        2 * mix.size * cells,
        lax.axis_index("core").reshape(1),
        both,
        cols,
        down_keep,
        down_more,
    )
    total = keep + lax.ppermute(give, "core", flip).astype(F32)
    total = swap(total.astype(BF16), ("z", "xh"))
    total = jnp.sum(total.astype(F32), axis=0) * scale
    grad_mix = total[:, : 9 * own_out].reshape(rows, 3, 3, own_out)
    piece = total[:, 9 * own_out : 11 * own_out].reshape(2, group, 2, own_out)
    grad_down = jnp.transpose(piece, (1, 2, 0, 3))

    (mixed,) = call(
        mixed_kernel, (shape((own_out, cells), BF16),), 2 * mix.size * cells, mix, both
    )
    mixed = mixed.reshape(own_out, n_rows, n_cols)

    turned = partial[:, pair_out:].reshape(n_chan, spare, own_out // spare, wide)
    turned = jnp.transpose(turned, (0, 2, 1, 3)).reshape(n_y, pair_out, wide)
    line = lax.axis_index("y")
    grad_image = sum(
        dot("dk,dq->kq", lax.dynamic_index_in_dim(turned, (line - k) % n_y, 0, False), near[k])
        for k in range(n_y)
    )
    grad_image = grad_image.astype(BF16).reshape(n_xl, taps, half)
    mine = jnp.where(first, grad_image[0], grad_image[1])
    theirs = lax.ppermute(jnp.where(first, grad_image[1], grad_image[0]), "xl", flip)
    grad_image = jnp.concatenate(
        [jnp.where(first, mine, theirs), jnp.where(first, theirs, mine)], axis=1
    )
    grad_image = grad_image.reshape(2, 2, own_in, n_rows, n_cols)
    grad_image = dot("abcrw,xbw->crax", grad_image, even_odd)
    grad_image = grad_image.astype(BF16).reshape(image.shape)
    return (mixed, grad_mix, grad_down, grad_image)


def solution(mesh):
    grid = mesh.devices
    n_chan, n_tile = grid.shape
    split = Mesh(grid.reshape(n_chan // 2, 2, n_tile // 4, 2, 2), CHAN + TILE)
    return jax.shard_map(
        per_device,
        mesh=split,
        in_specs=(
            P(CHAN, TILE, None),
            P(None, None, None, CHAN),
            P(None, None, None, CHAN),
            P(CHAN, TILE, None),
        ),
        out_specs=(
            P(CHAN, TILE, None),
            P(TILE, None, None, CHAN),
            P(TILE, None, None, CHAN),
            P(CHAN, TILE, None),
        ),
        check_vma=False,
    )
```

time: 147 us -> 143 us (0.973)
  waiting for transfers between devices: 48.6 us -> 35.2 us
  starting transfers between devices: 62.6 us -> 70.4 us
  local copies, waits for them, and re-layouts: 17.6 us -> 20.4 us
  Pallas kernels: 10.8 us -> 8.54 us
    all_to_all x5 -> x4, waiting for transfers between devices: 31 us -> 14.7 us  [swap(): return lax.all_to_all(block, axis, 0, 0)]
    ppermute x0 -> x3, starting transfers between devices: none -> 9.88 us  [per_device(): lax.ppermute(grad_pre, 'y', [(i, (i + k) % n_y) for i in range(n_y)])]
    unnamed x31 -> x35, local copies, waits for them, and re-layouts: 8.42 us -> 12.2 us
    pallas_call x4 -> x2, Pallas kernels: 8.56 us -> 5.12 us  [call_core(): pl.pallas_call(kernel, out_shape=tuple(outs), in_specs=[pl.BlockSpec(memo...]
    ppermute x1, starting transfers between devices: 5.15 us -> 1.92 us  [per_device(): below = lax.ppermute(cotangent[:, 0], TILE, back)]
    ppermute x1, waiting for transfers between devices: 3.21 us -> 6.36 us  [per_device(): below = lax.ppermute(cotangent[:, 0], TILE, back)]
    ppermute x1, waiting for transfers between devices: 2 us -> 4.62 us  [per_device(): lax.ppermute(jnp.where(first, grad_image[1], grad_image[0]), 'xl', flip)]
    broadcast_in_dim x1 -> x0, local copies, waits for them, and re-layouts: 1.77 us -> none  [per_device(): all_pre = jnp.broadcast_to(grad_pre[None], (n_y,) + grad_pre.shape)]
  transfers between devices with their start and end apart: 12 -> 14, of which waited for: 9 -> 5; matrix products, arithmetic and copies ran while one was open for 8% -> 10% of each run, Pallas kernels for 5% -> 3%
where the time goes in v4:
time: 143 us; the launch traced here: 142 us
  starting transfers between devices  70.4 us (49%)
  waiting for transfers between devices  35.2 us (25%)
  local copies, waits for them, and re-layouts  20.4 us (14%)
  Pallas kernels  8.54 us (6%)
  matrix products  3.59 us (3%)
  other arithmetic  2.5 us (2%)
    all_to_all x4, starting transfers between devices, swap(): return lax.all_to_all(block, axis, 0, 0)  39.4 us
    all_to_all x4, waiting for transfers between devices, swap(): return lax.all_to_all(block, axis, 0, 0)  14.7 us
    unnamed x35, local copies, waits for them, and re-layouts  12.2 us
    ppermute x3, starting transfers between devices, per_device(): lax.ppermute(grad_pre, 'y', [(i, (i + k) % n_y) for i in range(n_y)])  9.88 us
    ppermute x1, waiting for transfers between devices, per_device(): down_more = lax.ppermute(down_give, 'xl', flip)  7.84 us
    ppermute x1, waiting for transfers between devices, per_device(): below = lax.ppermute(cotangent[:, 0], TILE, back)  6.36 us
    pallas_call x2, Pallas kernels, call_core(): pl.pallas_call(kernel, out_shape=tuple(outs), in_specs=[pl.BlockSpec(memo...  5.12 us
    ppermute x1, waiting for transfers between devices, per_device(): lax.ppermute(jnp.where(first, grad_image[1], grad_image[0]), 'xl', flip)  4.62 us
  transfers between devices with their start and end apart: 14, of which 5 were waited for; matrix products, arithmetic and copies ran while one was open for 10% of the time, Pallas kernels for 3%

profile of v4, /device:TPU:4, one launch (start us, length us, event | category | flops | bytes accessed | tf_op | source)
XLA Modules:
  0.0 141.6 jit_solution(78201497099462339)
XLA Ops:
  3.5 5.2 %all-to-all-start = ((bf16[8,128,512]{2,1,0:T(8,128)(2,1)}), bf16[8,128,512]{2,1,0:T(8,128)(2,1)S(1)}, u32[]{:S(2)}, u32[]{:S(2)}) async-start(bf16[8,128,512]{2,1,0:T(8,128)(2,1)} %bitcast.9), calls=%async_computation | async-start | bytes 2097152 | tf_op jit(solution)/shard_map/all_to_all | solution.py:29
  9.6 3.9 %collective-permute-start.2 = (bf16[2,2,256,64]{3,2,1,0:T(8,128)(2,1)}, bf16[2,2,256,64]{3,2,1,0:T(8,128)(2,1)S(1)}, u32[]{:S(2)}, u32[]{:S(2)}) collective-permute-start(bf16[2,2,256,64]{3,2,1,0:T(8,128)(2,1)} %copy.36), channel_id=1, source_target_pairs={{0,64},{64,0},{1,65},{65,1},{2,66},{66,2},{3,67},{67,3},{4,68},{68... | collective-permute-start | bytes 393224 | tf_op jit(solution)/shard_map/ppermute | solution.py:233
  13.5 1.9 %collective-permute-start.1 = (bf16[64,128]{1,0:T(8,128)(2,1)S(1)}, bf16[64,128]{1,0:T(8,128)(2,1)S(1)}, u32[]{:S(2)}, u32[]{:S(2)}) collective-permute-start(bf16[64,128]{1,0:T(8,128)(2,1)S(1)} %get-tuple-element.48), channel_id=1, source_target_pairs={{1,0},{2,1},{3,2},{4,3},{5,4},{6,5},{7,6},{8,7},{9,8},{10,9},{11,1... | collective-permute-start | bytes 49160 | tf_op jit(solution)/shard_map/ppermute | solution.py:247
  15.5 2.4 %collective-permute-start = (bf16[64,128]{1,0:T(8,128)(2,1)S(1)}, bf16[64,128]{1,0:T(8,128)(2,1)S(1)}, u32[]{:S(2)}, u32[]{:S(2)}) collective-permute-start(bf16[64,128]{1,0:T(8,128)(2,1)S(1)} %get-tuple-element.49), channel_id=1, source_target_pairs={{0,1},{1,2},{2,3},{3,4},{4,5},{5,6},{6,7},{7,8},{8,9},{9,10},{10,1... | collective-permute-start | bytes 49160 | tf_op jit(solution)/shard_map/ppermute | solution.py:246
  19.6 6.4 %collective-permute-done.1.below_ref = bf16[64,128]{1,0:T(8,128)(2,1)S(1)} collective-permute-done((bf16[64,128]{1,0:T(8,128)(2,1)S(1)}, bf16[64,128]{1,0:T(8,128)(2,1)S(1)}, u32[]{:S(2)}, u32[]{:S(2)}) %collective-permute-start.1) | collective-permute-done | bytes 16416 | tf_op jit(solution)/shard_map/ppermute | solution.py:247
  31.3 5.4 %all-to-all-start.1 = ((bf16[8,160,512]{2,1,0:T(8,128)(2,1)}), bf16[8,160,512]{2,1,0:T(8,128)(2,1)S(1)}, u32[]{:S(2)}, u32[]{:S(2)}) async-start(bf16[8,160,512]{2,1,0:T(8,128)(2,1)} %copy-done.1), calls=%async_computation.1 | async-start | bytes 2621440 | tf_op jit(solution)/shard_map/all_to_all | solution.py:29
  38.2 1.6 %copy.38 = bf16[2,64,8,2,8,2,4]{1,0,6,5,4,3,2:T(2,128)(2,1)} copy(bf16[2,64,8,2,8,2,4]{1,6,4,2,5,3,0:T(4,128)(2,1)S(1)} %maximum_bitcast_fusion) | data formatting | bytes 524288 | tf_op jit(solution)/shard_map/transpose | solution.py:274
  39.8 2.0 %reshape.115 = bf16[128,1024]{0,1:T(8,128)(2,1)} reshape(bf16[2,64,8,2,8,2,4]{1,0,6,5,4,3,2:T(2,128)(2,1)} %copy.38) | data formatting | bytes 524288 | tf_op jit(solution)/shard_map/reshape | solution.py:274
  41.8 2.1 %fusion.7 = (f32[128,512]{1,0:T(8,128)}, bf16[128,512]{1,0:T(8,128)(2,1)S(1)}) fusion(bf16[128,1024]{0,1:T(8,128)(2,1)} %reshape.115, bf16[1024,512]{1,0:T(8,128)(2,1)S(1)} %bitcast.89), kind=kOutput, calls=%fused_computation.15 | convolution fusion | flops 134873088 | bytes 1703936 | tf_op jit(solution)/shard_map/dk,kq->dq/dot_general | solution.py:25
  43.9 4.4 %collective-permute-start.3 = (bf16[128,128]{1,0:T(8,128)(2,1)S(1)}, bf16[128,128]{1,0:T(8,128)(2,1)S(1)}, u32[]{:S(2)}, u32[]{:S(2)}) collective-permute-start(bf16[128,128]{1,0:T(8,128)(2,1)S(1)} %slice_select_fusion), channel_id=1, source_target_pairs={{1,0},{2,1},{3,2},{4,3},{5,4},{6,5},{7,6},{8,7},{9,8},{10,9},{11,1... | collective-permute-start | bytes 98312 | tf_op jit(solution)/shard_map/ppermute | solution.py:281
  48.4 1.6 %collective-permute-done.3.halo_ref = bf16[128,128]{1,0:T(8,128)(2,1)S(1)} collective-permute-done((bf16[128,128]{1,0:T(8,128)(2,1)S(1)}, bf16[128,128]{1,0:T(8,128)(2,1)S(1)}, u32[]{:S(2)}, u32[]{:S(2)}) %collective-permute-start.3) | collective-permute-done | bytes 32800 | tf_op jit(solution)/shard_map/ppermute | solution.py:281
  51.1 7.7 %all-to-all-start.2 = ((bf16[8,160,512]{2,1,0:T(8,128)(2,1)}), bf16[8,160,512]{2,1,0:T(8,128)(2,1)}, u32[]{:S(2)}, u32[]{:S(2)}) async-start(bf16[8,160,512]{2,1,0:T(8,128)(2,1)} %copy-done), calls=%async_computation.2 | async-start | bytes 2621440 | tf_op jit(solution)/shard_map/all_to_all | solution.py:29
  62.4 3.9 %collective-permute-start.4 = (bf16[512,128]{1,0:T(8,128)(2,1)}, bf16[512,128]{1,0:T(8,128)(2,1)S(1)}, u32[]{:S(2)}, u32[]{:S(2)}) collective-permute-start(bf16[512,128]{1,0:T(8,128)(2,1)} %get-tuple-element.30), channel_id=1, source_target_pairs={{0,64},{64,0},{1,65},{65,1},{2,66},{66,2},{3,67},{67,3},{4,68},{68... | collective-permute-start | bytes 393224 | tf_op jit(solution)/shard_map/ppermute | solution.py:304
  66.3 7.8 %collective-permute-done.4.more_ref = bf16[512,128]{1,0:T(8,128)(2,1)S(1)} collective-permute-done((bf16[512,128]{1,0:T(8,128)(2,1)}, bf16[512,128]{1,0:T(8,128)(2,1)S(1)}, u32[]{:S(2)}, u32[]{:S(2)}) %collective-permute-start.4) | collective-permute-done | bytes 131104 | tf_op jit(solution)/shard_map/ppermute | solution.py:304
  75.1 3.9 %shard_map.79 = (f32[32,8,768]{2,1,0:T(8,128)S(1)}, bf16[32,8,768]{2,1,0:T(8,128)(2,1)}) custom-call(s32[1]{0:T(128)} %bitcast.21.core_ref, bf16[8,160,512]{2,1,0:T(8,128)(2,1)} %all-to-all-done.2.both_ref, bf16[576,1024]{1,0:T(8,128)(2,1)S(1)} %get-tuple-element.26.cols_ref, f32[512,128]{1,0:T(8,128)S(1)} %copy-done.4, ...), custom_call_target="tpu_custom_call" | custom-call | flops 603979776 | bytes 4063232 | tf_op jit(solution)/shard_map/pallas_call | solution.py:55
  79.0 1.9 %collective-permute-start.5 = (bf16[32,8,768]{2,1,0:T(8,128)(2,1)}, bf16[32,8,768]{2,1,0:T(8,128)(2,1)S(1)}, u32[]{:S(2)}, u32[]{:S(2)}) collective-permute-start(bf16[32,8,768]{2,1,0:T(8,128)(2,1)} %get-tuple-element.32), channel_id=1, source_target_pairs={{0,1},{1,0},{2,3},{3,2},{4,5},{5,4},{6,7},{7,6},{8,9},{9,8},{10,11... | collective-permute-start | bytes 1179656 | tf_op jit(solution)/shard_map/ppermute | solution.py:325
  81.0 3.7 %collective-permute-start.8 = (bf16[128,512]{1,0:T(8,128)(2,1)S(1)}, bf16[128,512]{1,0:T(8,128)(2,1)S(1)}, u32[]{:S(2)}, u32[]{:S(2)}) collective-permute-start(bf16[128,512]{1,0:T(8,128)(2,1)S(1)} %copy-done.6), channel_id=1, source_target_pairs={{0,384},{128,0},{256,128},{384,256},{1,385},{129,1},{257,129},{385... | collective-permute-start | bytes 393224 | tf_op jit(solution)/shard_map/ppermute | solution.py:306
  84.7 2.8 %collective-permute-start.7 = (bf16[128,512]{1,0:T(8,128)(2,1)S(1)}, bf16[128,512]{1,0:T(8,128)(2,1)S(1)}, u32[]{:S(2)}, u32[]{:S(2)}) collective-permute-start(bf16[128,512]{1,0:T(8,128)(2,1)S(1)} %copy-done.6), channel_id=1, source_target_pairs={{0,256},{128,384},{256,0},{384,128},{1,257},{129,385},{257,1},{385... | collective-permute-start | bytes 393224 | tf_op jit(solution)/shard_map/ppermute | solution.py:306
  87.6 3.3 %collective-permute-start.6 = (bf16[128,512]{1,0:T(8,128)(2,1)S(1)}, bf16[128,512]{1,0:T(8,128)(2,1)S(1)}, u32[]{:S(2)}, u32[]{:S(2)}) collective-permute-start(bf16[128,512]{1,0:T(8,128)(2,1)S(1)} %copy-done.6), channel_id=1, source_target_pairs={{0,128},{128,256},{256,384},{384,0},{1,129},{129,257},{257,385},{3... | collective-permute-start | bytes 393224 | tf_op jit(solution)/shard_map/ppermute | solution.py:306
  92.0 21.1 %all-to-all-start.3 = ((bf16[32,8,768]{2,1,0:T(8,128)(2,1)}), bf16[32,8,768]{2,1,0:T(8,128)(2,1)S(1)}, u32[]{:S(2)}, u32[]{:S(2)}) async-start(bf16[32,8,768]{2,1,0:T(8,128)(2,1)} %add_convert_fusion), calls=%async_computation.3 | async-start | bytes 786432 | tf_op jit(solution)/shard_map/all_to_all | solution.py:29
  114.0 2.5 %collective-permute-start.9 = (bf16[128,512]{1,0:T(8,128)(2,1)S(1)}, bf16[128,512]{1,0:T(8,128)(2,1)S(1)}, u32[]{:S(2)}, u32[]{:S(2)}) collective-permute-start(bf16[128,512]{1,0:T(8,128)(2,1)S(1)} %broadcast_select_fusion.4), channel_id=1, source_target_pairs={{0,64},{64,0},{1,65},{65,1},{2,66},{66,2},{3,67},{67,3},{4,68},{68... | collective-permute-start | bytes 393224 | tf_op jit(solution)/shard_map/ppermute | solution.py:346
  116.5 4.6 %collective-permute-done.9 = bf16[128,512]{1,0:T(8,128)(2,1)S(1)} collective-permute-done((bf16[128,512]{1,0:T(8,128)(2,1)S(1)}, bf16[128,512]{1,0:T(8,128)(2,1)S(1)}, u32[]{:S(2)}, u32[]{:S(2)}) %collective-permute-start.9) | collective-permute-done | bytes 131104 | tf_op jit(solution)/shard_map/ppermute | solution.py:346
  122.4 2.2 %shard_map.77 = bf16[64,1024]{1,0:T(8,128)(2,1)S(1)} custom-call(bf16[576,512]{1,0:T(8,128)(2,1)S(1)} %bitcast.95, bf16[8,160,512]{2,1,0:T(8,128)(2,1)} %all-to-all-done.2.both_ref), custom_call_target="tpu_custom_call" | custom-call | flops 603979776 | bytes 2031616 | tf_op jit(solution)/shard_map/pallas_call | solution.py:42
  125.3 14.7 %all-to-all-done.3 = bf16[32,8,768]{2,1,0:T(8,128)(2,1)S(1)} async-done(((bf16[32,8,768]{2,1,0:T(8,128)(2,1)}), bf16[32,8,768]{2,1,0:T(8,128)(2,1)S(1)}, u32[]{:S(2)}, u32[]{:S(2)}) %all-to-all-start.3) | async-done | bytes 393248 | tf_op jit(solution)/shard_map/all_to_all | solution.py:29
  (81 shorter events, 23.2 us)
Async XLA Ops:
  3.5 5.2 %copy-start.13 = (bf16[2,2,256,64]{2,3,1,0:T(8,128)(2,1)S(1)}, bf16[2,2,256,64]{2,3,1,0:T(8,128)(2,1)}, u32[]{:S(2)}) copy-start(bf16[2,2,256,64]{2,3,1,0:T(8,128)(2,1)} %param.5) | copy-start | bytes 393220
  3.5 10.0 %copy-start.11 = (bf16[64,8,128]{2,1,0:T(8,128)(2,1)S(1)}, bf16[64,8,128]{2,1,0:T(8,128)(2,1)}, u32[]{:S(2)}) copy-start(bf16[64,8,128]{2,1,0:T(8,128)(2,1)} %param.7) | copy-start | bytes 393220
  3.5 27.1 %all-to-all-start = ((bf16[8,128,512]{2,1,0:T(8,128)(2,1)}), bf16[8,128,512]{2,1,0:T(8,128)(2,1)S(1)}, u32[]{:S(2)}, u32[]{:S(2)}) async-start(bf16[8,128,512]{2,1,0:T(8,128)(2,1)} %bitcast.9), calls=%async_computation | async-start | bytes 2097152 | tf_op jit(solution)/shard_map/all_to_all | solution.py:29
  9.6 21.0 %collective-permute-start.2 = (bf16[2,2,256,64]{3,2,1,0:T(8,128)(2,1)}, bf16[2,2,256,64]{3,2,1,0:T(8,128)(2,1)S(1)}, u32[]{:S(2)}, u32[]{:S(2)}) collective-permute-start(bf16[2,2,256,64]{3,2,1,0:T(8,128)(2,1)} %copy.36), channel_id=1, source_target_pairs={{0,64},{64,0},{1,65},{65,1},{2,66},{66,2},{3,67},{67,3},{4,68},{68... | collective-permute-start | bytes 393224 | tf_op jit(solution)/shard_map/ppermute | solution.py:233
  13.5 12.4 %collective-permute-start.1 = (bf16[64,128]{1,0:T(8,128)(2,1)S(1)}, bf16[64,128]{1,0:T(8,128)(2,1)S(1)}, u32[]{:S(2)}, u32[]{:S(2)}) collective-permute-start(bf16[64,128]{1,0:T(8,128)(2,1)S(1)} %get-tuple-element.48), channel_id=1, source_target_pairs={{1,0},{2,1},{3,2},{4,3},{5,4},{6,5},{7,6},{8,7},{9,8},{10,9},{11,1... | collective-permute-start | bytes 49160 | tf_op jit(solution)/shard_map/ppermute | solution.py:247
  15.5 10.5 %collective-permute-start = (bf16[64,128]{1,0:T(8,128)(2,1)S(1)}, bf16[64,128]{1,0:T(8,128)(2,1)S(1)}, u32[]{:S(2)}, u32[]{:S(2)}) collective-permute-start(bf16[64,128]{1,0:T(8,128)(2,1)S(1)} %get-tuple-element.49), channel_id=1, source_target_pairs={{0,1},{1,2},{2,3},{3,4},{4,5},{5,6},{6,7},{7,8},{8,9},{9,10},{10,1... | collective-permute-start | bytes 49160 | tf_op jit(solution)/shard_map/ppermute | solution.py:246
  26.5 1.1 copy-start.7
  29.5 1.1 copy-start.1
  30.6 0.7 copy-start.12
  31.3 19.8 %all-to-all-start.1 = ((bf16[8,160,512]{2,1,0:T(8,128)(2,1)}), bf16[8,160,512]{2,1,0:T(8,128)(2,1)S(1)}, u32[]{:S(2)}, u32[]{:S(2)}) async-start(bf16[8,160,512]{2,1,0:T(8,128)(2,1)} %copy-done.1), calls=%async_computation.1 | async-start | bytes 2621440 | tf_op jit(solution)/shard_map/all_to_all | solution.py:29
  43.9 6.0 %collective-permute-start.3 = (bf16[128,128]{1,0:T(8,128)(2,1)S(1)}, bf16[128,128]{1,0:T(8,128)(2,1)S(1)}, u32[]{:S(2)}, u32[]{:S(2)}) collective-permute-start(bf16[128,128]{1,0:T(8,128)(2,1)S(1)} %slice_select_fusion), channel_id=1, source_target_pairs={{1,0},{2,1},{3,2},{4,3},{5,4},{6,5},{7,6},{8,7},{9,8},{10,9},{11,1... | collective-permute-start | bytes 98312 | tf_op jit(solution)/shard_map/ppermute | solution.py:281
  50.0 1.1 copy-start
  51.1 23.1 %all-to-all-start.2 = ((bf16[8,160,512]{2,1,0:T(8,128)(2,1)}), bf16[8,160,512]{2,1,0:T(8,128)(2,1)}, u32[]{:S(2)}, u32[]{:S(2)}) async-start(bf16[8,160,512]{2,1,0:T(8,128)(2,1)} %copy-done), calls=%async_computation.2 | async-start | bytes 2621440 | tf_op jit(solution)/shard_map/all_to_all | solution.py:29
  58.8 0.9 copy-start.2
  62.4 11.8 %collective-permute-start.4 = (bf16[512,128]{1,0:T(8,128)(2,1)}, bf16[512,128]{1,0:T(8,128)(2,1)S(1)}, u32[]{:S(2)}, u32[]{:S(2)}) collective-permute-start(bf16[512,128]{1,0:T(8,128)(2,1)} %get-tuple-element.30), channel_id=1, source_target_pairs={{0,64},{64,0},{1,65},{65,1},{2,66},{66,2},{3,67},{67,3},{4,68},{68... | collective-permute-start | bytes 393224 | tf_op jit(solution)/shard_map/ppermute | solution.py:304
  74.2 1.0 copy-start.4
  75.1 5.9 %copy-start.6 = (bf16[128,512]{1,0:T(8,128)(2,1)S(1)}, bf16[128,512]{1,0:T(8,128)(2,1)}, u32[]{:S(2)}) copy-start(bf16[128,512]{1,0:T(8,128)(2,1)} %copy-done.5) | copy-start | bytes 393220
  79.0 12.2 %collective-permute-start.5 = (bf16[32,8,768]{2,1,0:T(8,128)(2,1)}, bf16[32,8,768]{2,1,0:T(8,128)(2,1)S(1)}, u32[]{:S(2)}, u32[]{:S(2)}) collective-permute-start(bf16[32,8,768]{2,1,0:T(8,128)(2,1)} %get-tuple-element.32), channel_id=1, source_target_pairs={{0,1},{1,0},{2,3},{3,2},{4,5},{5,4},{6,7},{7,6},{8,9},{9,8},{10,11... | collective-permute-start | bytes 1179656 | tf_op jit(solution)/shard_map/ppermute | solution.py:325
  81.0 32.5 %collective-permute-start.8 = (bf16[128,512]{1,0:T(8,128)(2,1)S(1)}, bf16[128,512]{1,0:T(8,128)(2,1)S(1)}, u32[]{:S(2)}, u32[]{:S(2)}) collective-permute-start(bf16[128,512]{1,0:T(8,128)(2,1)S(1)} %copy-done.6), channel_id=1, source_target_pairs={{0,384},{128,0},{256,128},{384,256},{1,385},{129,1},{257,129},{385... | collective-permute-start | bytes 393224 | tf_op jit(solution)/shard_map/ppermute | solution.py:306
  84.7 29.0 %collective-permute-start.7 = (bf16[128,512]{1,0:T(8,128)(2,1)S(1)}, bf16[128,512]{1,0:T(8,128)(2,1)S(1)}, u32[]{:S(2)}, u32[]{:S(2)}) collective-permute-start(bf16[128,512]{1,0:T(8,128)(2,1)S(1)} %copy-done.6), channel_id=1, source_target_pairs={{0,256},{128,384},{256,0},{384,128},{1,257},{129,385},{257,1},{385... | collective-permute-start | bytes 393224 | tf_op jit(solution)/shard_map/ppermute | solution.py:306
  87.6 25.6 %collective-permute-start.6 = (bf16[128,512]{1,0:T(8,128)(2,1)S(1)}, bf16[128,512]{1,0:T(8,128)(2,1)S(1)}, u32[]{:S(2)}, u32[]{:S(2)}) collective-permute-start(bf16[128,512]{1,0:T(8,128)(2,1)S(1)} %copy-done.6), channel_id=1, source_target_pairs={{0,128},{128,256},{256,384},{384,0},{1,129},{129,257},{257,385},{3... | collective-permute-start | bytes 393224 | tf_op jit(solution)/shard_map/ppermute | solution.py:306
  92.0 48.0 %all-to-all-start.3 = ((bf16[32,8,768]{2,1,0:T(8,128)(2,1)}), bf16[32,8,768]{2,1,0:T(8,128)(2,1)S(1)}, u32[]{:S(2)}, u32[]{:S(2)}) async-start(bf16[32,8,768]{2,1,0:T(8,128)(2,1)} %add_convert_fusion), calls=%async_computation.3 | async-start | bytes 786432 | tf_op jit(solution)/shard_map/all_to_all | solution.py:29
  114.0 7.2 %collective-permute-start.9 = (bf16[128,512]{1,0:T(8,128)(2,1)S(1)}, bf16[128,512]{1,0:T(8,128)(2,1)S(1)}, u32[]{:S(2)}, u32[]{:S(2)}) collective-permute-start(bf16[128,512]{1,0:T(8,128)(2,1)S(1)} %broadcast_select_fusion.4), channel_id=1, source_target_pairs={{0,64},{64,0},{1,65},{65,1},{2,66},{66,2},{3,67},{67,3},{4,68},{68... | collective-permute-start | bytes 393224 | tf_op jit(solution)/shard_map/ppermute | solution.py:346
  121.2 1.2 copy-start.8
  (4 other events, 2.7 us)

commit v5 on v4

--- a/solution.py
+++ b/solution.py
@@ -143,30 +143,102 @@
         give_ref[k * rows : (k + 1) * rows, :] = jnp.where(first, sides[1], sides[0]).astype(BF16)
 
 
-def grad_mix_kernel(core_ref, both_ref, cols_ref, down_ref, more_ref, keep_ref, give_ref):
+VM = pl.BlockSpec(memory_space=pltpu.VMEM)
+FAR = pl.BlockSpec(memory_space=pl.ANY)
+HBM = pl.BlockSpec(memory_space=pltpu.HBM)
+SM = pl.BlockSpec(memory_space=pltpu.SMEM)
+
+
+def run(kernel, in_specs, out_specs, outs, scratch, flops, *args):
+    size = sum(a.size * a.dtype.itemsize for a in args + tuple(outs))
+    return pl.pallas_call(
+        kernel,
+        out_shape=tuple(outs),
+        in_specs=in_specs,
+        out_specs=tuple(out_specs),
+        scratch_shapes=scratch,
+        cost_estimate=pl.CostEstimate(flops=flops, bytes_accessed=size, transcendentals=0),
+        compiler_params=pltpu.CompilerParams(vmem_limit_bytes=16 << 20),
+    )(*args)
+
+
+def grad_mix_kernel(
+    core_ref, both_hbm, cols_ref, down_hbm, more_hbm, keep_ref, give_hbm, hidden_ref, down_ref,
+    more_ref, give_ref, sems,
+):
     n_group, rows, width = keep_ref.shape
-    n_chan, _, half = both_ref.shape
-    taps, cells = cols_ref.shape
+    n_chan, _, half = both_hbm.shape
+    all_out, cells = hidden_ref.shape
+    taps = cols_ref.shape[0]
     n_half = cells // half
-    pair_out = n_group * 2 * rows * n_half // n_chan
+    pair_out = all_out * n_half // n_chan
+    maps = []
+    for k in range(n_chan):
+        y, h = divmod(k, n_half)
+        maps.append(
+            pltpu.make_async_copy(
+                both_hbm.at[k, pl.ds(0, pair_out)],
+                hidden_ref.at[pl.ds(y * pair_out, pair_out), pl.ds(h * half, half)],
+                sems.at[k],
+            )
+        )
+    downs = [
+        pltpu.make_async_copy(down_hbm, down_ref, sems.at[n_chan]),
+        pltpu.make_async_copy(more_hbm, more_ref, sems.at[n_chan + 1]),
+    ]
+    for copy in maps + downs:
+        copy.start()
     first = core_ref[0] == 0
-    step = pair_out // (2 * rows)
-    blank = jnp.zeros((pair_out, width - taps - down_ref.shape[1]), F32)
-    for y in range(n_chan // n_half):
-        hidden = jnp.concatenate(
-            [both_ref[y * n_half + h, :pair_out, :] for h in range(n_half)], axis=1
+    for copy in downs:
+        copy.wait()
+    parts = 2
+    size = all_out // parts
+    step = n_group // parts
+    blank = jnp.zeros((size, width - taps - down_ref.shape[1]), F32)
+    for part in range(parts):
+        for copy in maps[part * n_chan // parts : (part + 1) * n_chan // parts]:
+            copy.wait()
+        at = slice(part * size, (part + 1) * size)
+        total = lax.dot_general(
+            hidden_ref[at, :],
+            cols_ref[...],
+            (((1,), (1,)), ((), ())),
+            preferred_element_type=F32,
         )
-        total = lax.dot_general(
-            hidden, cols_ref[...], (((1,), (1,)), ((), ())), preferred_element_type=F32
-        )
-        at = slice(y * pair_out, (y + 1) * pair_out)
         extra = down_ref[at, :] + more_ref[at, :].astype(F32)
         total = jnp.concatenate([total, extra, blank], axis=1)
         total = total.reshape(step, 2, rows, width)
-        keep_ref[y * step : (y + 1) * step] = jnp.where(first, total[:, 0], total[:, 1])
-        give_ref[y * step : (y + 1) * step] = jnp.where(first, total[:, 1], total[:, 0]).astype(
-            BF16
-        )
+        to = slice(part * step, (part + 1) * step)
+        keep_ref[to] = jnp.where(first, total[:, 0], total[:, 1])
+        give_ref[to] = jnp.where(first, total[:, 1], total[:, 0]).astype(BF16)
+    give = pltpu.make_async_copy(give_ref, give_hbm, sems.at[n_chan + 2])
+    give.start()
+    give.wait()
+
+
+def grad_mix_parts(core, both, cols, down, more, n_tile, width):
+    n_chan, _, half = both.shape
+    all_out = down.shape[0]
+    rows = all_out // n_tile
+    return run(
+        grad_mix_kernel,
+        [SM, HBM, VM, FAR, FAR],
+        [VM, FAR],
+        (shape((n_tile // 2, rows, width), F32), shape((n_tile // 2, rows, width), BF16)),
+        [
+            pltpu.VMEM((all_out, cols.shape[1]), BF16),
+            pltpu.VMEM(down.shape, F32),
+            pltpu.VMEM(down.shape, BF16),
+            pltpu.VMEM((n_tile // 2, rows, width), BF16),
+            pltpu.SemaphoreType.DMA((n_chan + 3,)),
+        ],
+        2 * all_out * cols.size,
+        core,
+        both,
+        cols,
+        down,
+        more,
+    )
 
 
 def mixed_kernel(mix_ref, both_ref, out_ref):
@@ -309,19 +381,8 @@
 
     rows = all_out // n_tile
     width = 12 * own_out
-    keep, give = call_core(
-        grad_mix_kernel,
-        (
-            shape((n_z * n_xh, rows, width), F32),
-            shape((n_z * n_xh, rows, width), BF16),
-        ),
-        2 * mix.size * cells,
-        lax.axis_index("core").reshape(1),
-        both,
-        cols,
-        down_keep,
-        down_more,
-    )
+    core = lax.axis_index("core").reshape(1)
+    keep, give = grad_mix_parts(core, both, cols, down_keep, down_more, n_tile, width)
     total = keep + lax.ppermute(give, "core", flip).astype(F32)
     total = swap(total.astype(BF16), ("z", "xh"))
     total = jnp.sum(total.astype(F32), axis=0) * scale

time: 143 us -> 142 us (level)
    pallas_call x2 -> x1, Pallas kernels: 5.12 us -> 1.26 us  [call_core(): pl.pallas_call(kernel, out_shape=tuple(outs), in_specs=[pl.BlockSpec(memo...]
    pallas_call x0 -> x1, Pallas kernels: none -> 3.48 us  [run(): pl.pallas_call(kernel, out_shape=tuple(outs), in_specs=in_specs, out_spec...]
where the time goes in v5:
time: 142 us; the launch traced here: 141 us
  starting transfers between devices  70.4 us (50%)
  waiting for transfers between devices  35.1 us (25%)
  local copies, waits for them, and re-layouts  20.4 us (14%)
  Pallas kernels  8.16 us (6%)
  matrix products  3.59 us (3%)
  other arithmetic  2.5 us (2%)
    all_to_all x4, starting transfers between devices, swap(): return lax.all_to_all(block, axis, 0, 0)  39.4 us
    all_to_all x4, waiting for transfers between devices, swap(): return lax.all_to_all(block, axis, 0, 0)  14.8 us
    unnamed x35, local copies, waits for them, and re-layouts  12.2 us
    ppermute x3, starting transfers between devices, per_device(): lax.ppermute(grad_pre, 'y', [(i, (i + k) % n_y) for i in range(n_y)])  9.88 us
    ppermute x1, waiting for transfers between devices, per_device(): down_more = lax.ppermute(down_give, 'xl', flip)  7.84 us
    ppermute x1, waiting for transfers between devices, per_device(): below = lax.ppermute(cotangent[:, 0], TILE, back)  6.36 us
    ppermute x1, waiting for transfers between devices, per_device(): lax.ppermute(jnp.where(first, grad_image[1], grad_image[0]), 'xl', flip)  4.57 us
    ppermute x1, starting transfers between devices, per_device(): lax.ppermute(halo, ('xl',) + TILE, back + [(n_tile + i, n_tile + j) for i...  4.44 us
  transfers between devices with their start and end apart: 14, of which 5 were waited for; matrix products, arithmetic and copies ran while one was open for 10% of the time, Pallas kernels for 3%

profile of v5, /device:TPU:4, one launch (start us, length us, event | category | flops | bytes accessed | tf_op | source)
XLA Modules:
  0.0 141.3 jit_solution(5569364973184060338)
XLA Ops:
  3.5 5.2 %all-to-all-start = ((bf16[8,128,512]{2,1,0:T(8,128)(2,1)}), bf16[8,128,512]{2,1,0:T(8,128)(2,1)S(1)}, u32[]{:S(2)}, u32[]{:S(2)}) async-start(bf16[8,128,512]{2,1,0:T(8,128)(2,1)} %bitcast.9), calls=%async_computation | async-start | bytes 2097152 | tf_op jit(solution)/shard_map/all_to_all | solution.py:29
  9.6 3.9 %collective-permute-start.2 = (bf16[2,2,256,64]{3,2,1,0:T(8,128)(2,1)}, bf16[2,2,256,64]{3,2,1,0:T(8,128)(2,1)S(1)}, u32[]{:S(2)}, u32[]{:S(2)}) collective-permute-start(bf16[2,2,256,64]{3,2,1,0:T(8,128)(2,1)} %copy.36), channel_id=1, source_target_pairs={{0,64},{64,0},{1,65},{65,1},{2,66},{66,2},{3,67},{67,3},{4,68},{68... | collective-permute-start | bytes 393224 | tf_op jit(solution)/shard_map/ppermute | solution.py:305
  13.5 1.9 %collective-permute-start.1 = (bf16[64,128]{1,0:T(8,128)(2,1)S(1)}, bf16[64,128]{1,0:T(8,128)(2,1)S(1)}, u32[]{:S(2)}, u32[]{:S(2)}) collective-permute-start(bf16[64,128]{1,0:T(8,128)(2,1)S(1)} %get-tuple-element.48), channel_id=1, source_target_pairs={{1,0},{2,1},{3,2},{4,3},{5,4},{6,5},{7,6},{8,7},{9,8},{10,9},{11,1... | collective-permute-start | bytes 49160 | tf_op jit(solution)/shard_map/ppermute | solution.py:319
  15.5 2.4 %collective-permute-start = (bf16[64,128]{1,0:T(8,128)(2,1)S(1)}, bf16[64,128]{1,0:T(8,128)(2,1)S(1)}, u32[]{:S(2)}, u32[]{:S(2)}) collective-permute-start(bf16[64,128]{1,0:T(8,128)(2,1)S(1)} %get-tuple-element.49), channel_id=1, source_target_pairs={{0,1},{1,2},{2,3},{3,4},{4,5},{5,6},{6,7},{7,8},{8,9},{9,10},{10,1... | collective-permute-start | bytes 49160 | tf_op jit(solution)/shard_map/ppermute | solution.py:318
  19.6 6.4 %collective-permute-done.1.below_ref = bf16[64,128]{1,0:T(8,128)(2,1)S(1)} collective-permute-done((bf16[64,128]{1,0:T(8,128)(2,1)S(1)}, bf16[64,128]{1,0:T(8,128)(2,1)S(1)}, u32[]{:S(2)}, u32[]{:S(2)}) %collective-permute-start.1) | collective-permute-done | bytes 16416 | tf_op jit(solution)/shard_map/ppermute | solution.py:319
  31.3 5.4 %all-to-all-start.1 = ((bf16[8,160,512]{2,1,0:T(8,128)(2,1)}), bf16[8,160,512]{2,1,0:T(8,128)(2,1)S(1)}, u32[]{:S(2)}, u32[]{:S(2)}) async-start(bf16[8,160,512]{2,1,0:T(8,128)(2,1)} %copy-done.1), calls=%async_computation.1 | async-start | bytes 2621440 | tf_op jit(solution)/shard_map/all_to_all | solution.py:29
  38.2 1.6 %copy.38 = bf16[2,64,8,2,8,2,4]{1,0,6,5,4,3,2:T(2,128)(2,1)} copy(bf16[2,64,8,2,8,2,4]{1,6,4,2,5,3,0:T(4,128)(2,1)S(1)} %maximum_bitcast_fusion) | data formatting | bytes 524288 | tf_op jit(solution)/shard_map/transpose | solution.py:346
  39.8 2.0 %reshape.115 = bf16[128,1024]{0,1:T(8,128)(2,1)} reshape(bf16[2,64,8,2,8,2,4]{1,0,6,5,4,3,2:T(2,128)(2,1)} %copy.38) | data formatting | bytes 524288 | tf_op jit(solution)/shard_map/reshape | solution.py:346
  41.8 2.1 %fusion.7 = (f32[128,512]{1,0:T(8,128)}, bf16[128,512]{1,0:T(8,128)(2,1)S(1)}) fusion(bf16[128,1024]{0,1:T(8,128)(2,1)} %reshape.115, bf16[1024,512]{1,0:T(8,128)(2,1)S(1)} %bitcast.89), kind=kOutput, calls=%fused_computation.15 | convolution fusion | flops 134873088 | bytes 1703936 | tf_op jit(solution)/shard_map/dk,kq->dq/dot_general | solution.py:25
  43.9 4.4 %collective-permute-start.3 = (bf16[128,128]{1,0:T(8,128)(2,1)S(1)}, bf16[128,128]{1,0:T(8,128)(2,1)S(1)}, u32[]{:S(2)}, u32[]{:S(2)}) collective-permute-start(bf16[128,128]{1,0:T(8,128)(2,1)S(1)} %slice_select_fusion), channel_id=1, source_target_pairs={{1,0},{2,1},{3,2},{4,3},{5,4},{6,5},{7,6},{8,7},{9,8},{10,9},{11,1... | collective-permute-start | bytes 98312 | tf_op jit(solution)/shard_map/ppermute | solution.py:353
  48.4 1.6 %collective-permute-done.3.halo_ref = bf16[128,128]{1,0:T(8,128)(2,1)S(1)} collective-permute-done((bf16[128,128]{1,0:T(8,128)(2,1)S(1)}, bf16[128,128]{1,0:T(8,128)(2,1)S(1)}, u32[]{:S(2)}, u32[]{:S(2)}) %collective-permute-start.3) | collective-permute-done | bytes 32800 | tf_op jit(solution)/shard_map/ppermute | solution.py:353
  51.1 7.7 %all-to-all-start.2 = ((bf16[8,160,512]{2,1,0:T(8,128)(2,1)}), bf16[8,160,512]{2,1,0:T(8,128)(2,1)}, u32[]{:S(2)}, u32[]{:S(2)}) async-start(bf16[8,160,512]{2,1,0:T(8,128)(2,1)} %copy-done), calls=%async_computation.2 | async-start | bytes 2621440 | tf_op jit(solution)/shard_map/all_to_all | solution.py:29
  62.4 3.9 %collective-permute-start.4 = (bf16[512,128]{1,0:T(8,128)(2,1)}, bf16[512,128]{1,0:T(8,128)(2,1)S(1)}, u32[]{:S(2)}, u32[]{:S(2)}) collective-permute-start(bf16[512,128]{1,0:T(8,128)(2,1)} %get-tuple-element.30), channel_id=1, source_target_pairs={{0,64},{64,0},{1,65},{65,1},{2,66},{66,2},{3,67},{67,3},{4,68},{68... | collective-permute-start | bytes 393224 | tf_op jit(solution)/shard_map/ppermute | solution.py:376
  66.3 7.8 %collective-permute-done.4.more_hbm = bf16[512,128]{1,0:T(8,128)(2,1)S(1)} collective-permute-done((bf16[512,128]{1,0:T(8,128)(2,1)}, bf16[512,128]{1,0:T(8,128)(2,1)S(1)}, u32[]{:S(2)}, u32[]{:S(2)}) %collective-permute-start.4) | collective-permute-done | bytes 131104 | tf_op jit(solution)/shard_map/ppermute | solution.py:376
  75.1 3.5 %shard_map.79 = (f32[32,8,768]{2,1,0:T(8,128)S(1)}, bf16[32,8,768]{2,1,0:T(8,128)(2,1)}) custom-call(s32[1]{0:T(128)} %bitcast.21.core_ref, bf16[8,160,512]{2,1,0:T(8,128)(2,1)} %all-to-all-done.2.both_ref.both_hbm, bf16[576,1024]{1,0:T(8,128)(2,1)S(1)} %get-tuple-element.26.cols_ref, f32[512,128]{1,0:T(8,128)S(1)} %copy-done.4, ...), custom_call_target="tpu_custom_call" | custom-call | flops 603979776 | bytes 4063236 | tf_op jit(solution)/shard_map/pallas_call | solution.py:154
  78.6 1.9 %collective-permute-start.5 = (bf16[32,8,768]{2,1,0:T(8,128)(2,1)}, bf16[32,8,768]{2,1,0:T(8,128)(2,1)S(1)}, u32[]{:S(2)}, u32[]{:S(2)}) collective-permute-start(bf16[32,8,768]{2,1,0:T(8,128)(2,1)} %get-tuple-element.32), channel_id=1, source_target_pairs={{0,1},{1,0},{2,3},{3,2},{4,5},{5,4},{6,7},{7,6},{8,9},{9,8},{10,11... | collective-permute-start | bytes 1179656 | tf_op jit(solution)/shard_map/ppermute | solution.py:386
  80.6 3.7 %collective-permute-start.8 = (bf16[128,512]{1,0:T(8,128)(2,1)S(1)}, bf16[128,512]{1,0:T(8,128)(2,1)S(1)}, u32[]{:S(2)}, u32[]{:S(2)}) collective-permute-start(bf16[128,512]{1,0:T(8,128)(2,1)S(1)} %copy-done.6), channel_id=1, source_target_pairs={{0,384},{128,0},{256,128},{384,256},{1,385},{129,1},{257,129},{385... | collective-permute-start | bytes 393224 | tf_op jit(solution)/shard_map/ppermute | solution.py:378
  84.4 2.8 %collective-permute-start.7 = (bf16[128,512]{1,0:T(8,128)(2,1)S(1)}, bf16[128,512]{1,0:T(8,128)(2,1)S(1)}, u32[]{:S(2)}, u32[]{:S(2)}) collective-permute-start(bf16[128,512]{1,0:T(8,128)(2,1)S(1)} %copy-done.6), channel_id=1, source_target_pairs={{0,256},{128,384},{256,0},{384,128},{1,257},{129,385},{257,1},{385... | collective-permute-start | bytes 393224 | tf_op jit(solution)/shard_map/ppermute | solution.py:378
  87.2 3.3 %collective-permute-start.6 = (bf16[128,512]{1,0:T(8,128)(2,1)S(1)}, bf16[128,512]{1,0:T(8,128)(2,1)S(1)}, u32[]{:S(2)}, u32[]{:S(2)}) collective-permute-start(bf16[128,512]{1,0:T(8,128)(2,1)S(1)} %copy-done.6), channel_id=1, source_target_pairs={{0,128},{128,256},{256,384},{384,0},{1,129},{129,257},{257,385},{3... | collective-permute-start | bytes 393224 | tf_op jit(solution)/shard_map/ppermute | solution.py:378
  91.7 21.1 %all-to-all-start.3 = ((bf16[32,8,768]{2,1,0:T(8,128)(2,1)}), bf16[32,8,768]{2,1,0:T(8,128)(2,1)S(1)}, u32[]{:S(2)}, u32[]{:S(2)}) async-start(bf16[32,8,768]{2,1,0:T(8,128)(2,1)} %add_convert_fusion), calls=%async_computation.3 | async-start | bytes 786432 | tf_op jit(solution)/shard_map/all_to_all | solution.py:29
  113.7 2.6 %collective-permute-start.9 = (bf16[128,512]{1,0:T(8,128)(2,1)S(1)}, bf16[128,512]{1,0:T(8,128)(2,1)S(1)}, u32[]{:S(2)}, u32[]{:S(2)}) collective-permute-start(bf16[128,512]{1,0:T(8,128)(2,1)S(1)} %broadcast_select_fusion.4), channel_id=1, source_target_pairs={{0,64},{64,0},{1,65},{65,1},{2,66},{66,2},{3,67},{67,3},{4,68},{68... | collective-permute-start | bytes 393224 | tf_op jit(solution)/shard_map/ppermute | solution.py:407
  116.2 4.6 %collective-permute-done.9 = bf16[128,512]{1,0:T(8,128)(2,1)S(1)} collective-permute-done((bf16[128,512]{1,0:T(8,128)(2,1)S(1)}, bf16[128,512]{1,0:T(8,128)(2,1)S(1)}, u32[]{:S(2)}, u32[]{:S(2)}) %collective-permute-start.9) | collective-permute-done | bytes 131104 | tf_op jit(solution)/shard_map/ppermute | solution.py:407
  122.1 2.2 %shard_map.77 = bf16[64,1024]{1,0:T(8,128)(2,1)S(1)} custom-call(bf16[576,512]{1,0:T(8,128)(2,1)S(1)} %bitcast.95, bf16[8,160,512]{2,1,0:T(8,128)(2,1)} %all-to-all-done.2.both_ref.both_hbm), custom_call_target="tpu_custom_call" | custom-call | flops 603979776 | bytes 2031616 | tf_op jit(solution)/shard_map/pallas_call | solution.py:42
  125.0 14.7 %all-to-all-done.3 = bf16[32,8,768]{2,1,0:T(8,128)(2,1)S(1)} async-done(((bf16[32,8,768]{2,1,0:T(8,128)(2,1)}), bf16[32,8,768]{2,1,0:T(8,128)(2,1)S(1)}, u32[]{:S(2)}, u32[]{:S(2)}) %all-to-all-start.3) | async-done | bytes 393248 | tf_op jit(solution)/shard_map/all_to_all | solution.py:29
  (81 shorter events, 23.2 us)
Async XLA Ops:
  3.5 5.2 %copy-start.13 = (bf16[2,2,256,64]{2,3,1,0:T(8,128)(2,1)S(1)}, bf16[2,2,256,64]{2,3,1,0:T(8,128)(2,1)}, u32[]{:S(2)}) copy-start(bf16[2,2,256,64]{2,3,1,0:T(8,128)(2,1)} %param.5) | copy-start | bytes 393220
  3.5 10.0 %copy-start.11 = (bf16[64,8,128]{2,1,0:T(8,128)(2,1)S(1)}, bf16[64,8,128]{2,1,0:T(8,128)(2,1)}, u32[]{:S(2)}) copy-start(bf16[64,8,128]{2,1,0:T(8,128)(2,1)} %param.7) | copy-start | bytes 393220
  3.5 27.1 %all-to-all-start = ((bf16[8,128,512]{2,1,0:T(8,128)(2,1)}), bf16[8,128,512]{2,1,0:T(8,128)(2,1)S(1)}, u32[]{:S(2)}, u32[]{:S(2)}) async-start(bf16[8,128,512]{2,1,0:T(8,128)(2,1)} %bitcast.9), calls=%async_computation | async-start | bytes 2097152 | tf_op jit(solution)/shard_map/all_to_all | solution.py:29
  9.6 21.0 %collective-permute-start.2 = (bf16[2,2,256,64]{3,2,1,0:T(8,128)(2,1)}, bf16[2,2,256,64]{3,2,1,0:T(8,128)(2,1)S(1)}, u32[]{:S(2)}, u32[]{:S(2)}) collective-permute-start(bf16[2,2,256,64]{3,2,1,0:T(8,128)(2,1)} %copy.36), channel_id=1, source_target_pairs={{0,64},{64,0},{1,65},{65,1},{2,66},{66,2},{3,67},{67,3},{4,68},{68... | collective-permute-start | bytes 393224 | tf_op jit(solution)/shard_map/ppermute | solution.py:305
  13.5 12.4 %collective-permute-start.1 = (bf16[64,128]{1,0:T(8,128)(2,1)S(1)}, bf16[64,128]{1,0:T(8,128)(2,1)S(1)}, u32[]{:S(2)}, u32[]{:S(2)}) collective-permute-start(bf16[64,128]{1,0:T(8,128)(2,1)S(1)} %get-tuple-element.48), channel_id=1, source_target_pairs={{1,0},{2,1},{3,2},{4,3},{5,4},{6,5},{7,6},{8,7},{9,8},{10,9},{11,1... | collective-permute-start | bytes 49160 | tf_op jit(solution)/shard_map/ppermute | solution.py:319
  15.5 10.5 %collective-permute-start = (bf16[64,128]{1,0:T(8,128)(2,1)S(1)}, bf16[64,128]{1,0:T(8,128)(2,1)S(1)}, u32[]{:S(2)}, u32[]{:S(2)}) collective-permute-start(bf16[64,128]{1,0:T(8,128)(2,1)S(1)} %get-tuple-element.49), channel_id=1, source_target_pairs={{0,1},{1,2},{2,3},{3,4},{4,5},{5,6},{6,7},{7,8},{8,9},{9,10},{10,1... | collective-permute-start | bytes 49160 | tf_op jit(solution)/shard_map/ppermute | solution.py:318
  26.5 1.1 copy-start.7
  29.5 1.1 copy-start.1
  30.6 0.7 copy-start.12
  31.3 19.8 %all-to-all-start.1 = ((bf16[8,160,512]{2,1,0:T(8,128)(2,1)}), bf16[8,160,512]{2,1,0:T(8,128)(2,1)S(1)}, u32[]{:S(2)}, u32[]{:S(2)}) async-start(bf16[8,160,512]{2,1,0:T(8,128)(2,1)} %copy-done.1), calls=%async_computation.1 | async-start | bytes 2621440 | tf_op jit(solution)/shard_map/all_to_all | solution.py:29
  43.9 6.0 %collective-permute-start.3 = (bf16[128,128]{1,0:T(8,128)(2,1)S(1)}, bf16[128,128]{1,0:T(8,128)(2,1)S(1)}, u32[]{:S(2)}, u32[]{:S(2)}) collective-permute-start(bf16[128,128]{1,0:T(8,128)(2,1)S(1)} %slice_select_fusion), channel_id=1, source_target_pairs={{1,0},{2,1},{3,2},{4,3},{5,4},{6,5},{7,6},{8,7},{9,8},{10,9},{11,1... | collective-permute-start | bytes 98312 | tf_op jit(solution)/shard_map/ppermute | solution.py:353
  50.0 1.1 copy-start
  51.1 23.1 %all-to-all-start.2 = ((bf16[8,160,512]{2,1,0:T(8,128)(2,1)}), bf16[8,160,512]{2,1,0:T(8,128)(2,1)}, u32[]{:S(2)}, u32[]{:S(2)}) async-start(bf16[8,160,512]{2,1,0:T(8,128)(2,1)} %copy-done), calls=%async_computation.2 | async-start | bytes 2621440 | tf_op jit(solution)/shard_map/all_to_all | solution.py:29
  58.8 0.9 copy-start.2
  62.4 11.8 %collective-permute-start.4 = (bf16[512,128]{1,0:T(8,128)(2,1)}, bf16[512,128]{1,0:T(8,128)(2,1)S(1)}, u32[]{:S(2)}, u32[]{:S(2)}) collective-permute-start(bf16[512,128]{1,0:T(8,128)(2,1)} %get-tuple-element.30), channel_id=1, source_target_pairs={{0,64},{64,0},{1,65},{65,1},{2,66},{66,2},{3,67},{67,3},{4,68},{68... | collective-permute-start | bytes 393224 | tf_op jit(solution)/shard_map/ppermute | solution.py:376
  74.2 1.0 copy-start.4
  75.1 5.5 %copy-start.6 = (bf16[128,512]{1,0:T(8,128)(2,1)S(1)}, bf16[128,512]{1,0:T(8,128)(2,1)}, u32[]{:S(2)}) copy-start(bf16[128,512]{1,0:T(8,128)(2,1)} %copy-done.5) | copy-start | bytes 393220
  78.6 12.2 %collective-permute-start.5 = (bf16[32,8,768]{2,1,0:T(8,128)(2,1)}, bf16[32,8,768]{2,1,0:T(8,128)(2,1)S(1)}, u32[]{:S(2)}, u32[]{:S(2)}) collective-permute-start(bf16[32,8,768]{2,1,0:T(8,128)(2,1)} %get-tuple-element.32), channel_id=1, source_target_pairs={{0,1},{1,0},{2,3},{3,2},{4,5},{5,4},{6,7},{7,6},{8,9},{9,8},{10,11... | collective-permute-start | bytes 1179656 | tf_op jit(solution)/shard_map/ppermute | solution.py:386
  80.6 32.5 %collective-permute-start.8 = (bf16[128,512]{1,0:T(8,128)(2,1)S(1)}, bf16[128,512]{1,0:T(8,128)(2,1)S(1)}, u32[]{:S(2)}, u32[]{:S(2)}) collective-permute-start(bf16[128,512]{1,0:T(8,128)(2,1)S(1)} %copy-done.6), channel_id=1, source_target_pairs={{0,384},{128,0},{256,128},{384,256},{1,385},{129,1},{257,129},{385... | collective-permute-start | bytes 393224 | tf_op jit(solution)/shard_map/ppermute | solution.py:378
  84.4 29.0 %collective-permute-start.7 = (bf16[128,512]{1,0:T(8,128)(2,1)S(1)}, bf16[128,512]{1,0:T(8,128)(2,1)S(1)}, u32[]{:S(2)}, u32[]{:S(2)}) collective-permute-start(bf16[128,512]{1,0:T(8,128)(2,1)S(1)} %copy-done.6), channel_id=1, source_target_pairs={{0,256},{128,384},{256,0},{384,128},{1,257},{129,385},{257,1},{385... | collective-permute-start | bytes 393224 | tf_op jit(solution)/shard_map/ppermute | solution.py:378
  87.2 25.6 %collective-permute-start.6 = (bf16[128,512]{1,0:T(8,128)(2,1)S(1)}, bf16[128,512]{1,0:T(8,128)(2,1)S(1)}, u32[]{:S(2)}, u32[]{:S(2)}) collective-permute-start(bf16[128,512]{1,0:T(8,128)(2,1)S(1)} %copy-done.6), channel_id=1, source_target_pairs={{0,128},{128,256},{256,384},{384,0},{1,129},{129,257},{257,385},{3... | collective-permute-start | bytes 393224 | tf_op jit(solution)/shard_map/ppermute | solution.py:378
  91.7 48.0 %all-to-all-start.3 = ((bf16[32,8,768]{2,1,0:T(8,128)(2,1)}), bf16[32,8,768]{2,1,0:T(8,128)(2,1)S(1)}, u32[]{:S(2)}, u32[]{:S(2)}) async-start(bf16[32,8,768]{2,1,0:T(8,128)(2,1)} %add_convert_fusion), calls=%async_computation.3 | async-start | bytes 786432 | tf_op jit(solution)/shard_map/all_to_all | solution.py:29
  113.7 7.1 %collective-permute-start.9 = (bf16[128,512]{1,0:T(8,128)(2,1)S(1)}, bf16[128,512]{1,0:T(8,128)(2,1)S(1)}, u32[]{:S(2)}, u32[]{:S(2)}) collective-permute-start(bf16[128,512]{1,0:T(8,128)(2,1)S(1)} %broadcast_select_fusion.4), channel_id=1, source_target_pairs={{0,64},{64,0},{1,65},{65,1},{2,66},{66,2},{3,67},{67,3},{4,68},{68... | collective-permute-start | bytes 393224 | tf_op jit(solution)/shard_map/ppermute | solution.py:407
  120.8 1.2 copy-start.8
  (4 other events, 2.7 us)
